TPU v7x, 32 devices: a whole 2x2x4 slice. The times are simulated.
32 devices in a mesh: dp: 2 (over x), fsdp: 16 (over z, y, core).
Axes of the slice: x: 2, y: 2, z: 4, core: 2. Of those that a mesh axis runs over, the one named last changes fastest.
Arguments:
- image_tokens: bfloat16 [1024, 50, 768], P(('dp', 'fsdp')), may hold values from -6 to 6
- text_tokens: bfloat16 [1024, 16, 768], P(('dp', 'fsdp')), may hold values from -6 to 6
- image_qkv: bfloat16 [768, 2304], replicated, may hold values from -0.21875 to 0.21875
- image_out: bfloat16 [768, 768], replicated, may hold values from -1.25 to 1.25
- image_up: bfloat16 [768, 3072], replicated, may hold values from -0.21875 to 0.21875
- image_down: bfloat16 [3072, 768], replicated, may hold values from -0.109375 to 0.109375
- image_vectors: bfloat16 [8, 768], replicated, may hold values from -1.2 to 1.5
- image_up_bias: bfloat16 [3072], replicated, may hold values from -2 to 2
- text_qkv: bfloat16 [768, 2304], P('fsdp', 'dp'), may hold values from -0.21875 to 0.21875
- text_out: bfloat16 [768, 768], P('fsdp', 'dp'), may hold values from -0.875 to 0.875
- text_up: bfloat16 [768, 3072], P('fsdp', 'dp'), may hold values from -0.21875 to 0.21875
- text_down: bfloat16 [3072, 768], P('fsdp', 'dp'), may hold values from -0.109375 to 0.109375
- text_vectors: bfloat16 [8, 768], P(None, 'fsdp'), may hold values from -1.2 to 1.5
- text_up_bias: bfloat16 [3072], P('fsdp'), may hold values from -2 to 2
- pair_counts: int32 [32], replicated, may hold values from 8 to 32, as said below
- pair_groups: int32 [1024], replicated, may hold values from 0 to 511
Outputs:
- loss_value: float32 [], replicated
- grad_text_tokens: float32 [1024, 16, 768], P(('dp', 'fsdp'))
- grad_text_qkv: float32 [768, 2304], P('fsdp', 'dp')
- grad_text_out: float32 [768, 768], P('fsdp', 'dp')
- grad_text_up: float32 [768, 3072], P('fsdp', 'dp')
- grad_text_down: float32 [3072, 768], P('fsdp', 'dp')
- grad_text_vectors: float32 [8, 768], P(None, 'fsdp')
- grad_text_up_bias: float32 [3072], P('fsdp')
Inputs may be any that keep to these rules, and one draw needn't show every extreme that they name: Device d (index over dp+fsdp, dp slowest) has its first pair_counts[d] of its 32 pair slots live; some device is full.
All inputs are finite; a program needn't handle non-finite values.
Results may differ from a plain program's by a relative error of at most 0.024.
Values may be sent and summed in bfloat16 or wider, within the bound.
No kernel may reach another device: no remote copies, remote signals or barrier semaphores. Data moves between devices by JAX's collectives and lax.ppermute only.
A program may use at most 192 MiB of HBM per device.

v0:
```python
import functools

import jax
import jax.numpy as jnp
from jax import lax
from jax.experimental import pallas as pl
from jax.experimental.pallas import tpu as pltpu
from jax.sharding import PartitionSpec as P

HEAD_DIM = 64
LOGIT_SCALE = 50.0
LOSS_WEIGHT = 32768.0
BF = jnp.bfloat16
F32 = jnp.float32
AXES = ("dp", "fsdp")
PX, PF = 2, 16

ANY = pl.BlockSpec(memory_space=pltpu.HBM)
WHOLE = pl.BlockSpec(memory_space=pltpu.VMEM)


def params(mebibytes=62):
    return pltpu.CompilerParams(vmem_limit_bytes=mebibytes * 1024 * 1024)


def dot(a, b, ca=1, cb=0):
    return lax.dot_general(a, b, (((ca,), (cb,)), ((), ())), preferred_element_type=F32)


def repeat(count, step, together=1):
    def turn(j, _):
        for k in range(together):
            step(j * together + k)
        return 0

    if together >= count:
        for i in range(count):
            step(i)
    else:
        lax.fori_loop(0, count // together, turn, 0)


def move(pairs, sem, base=0):
    copies = [pltpu.make_async_copy(a, b, sem.at[base + i]) for i, (a, b) in enumerate(pairs)]
    for copy in copies:
        copy.start()
    return copies


def normalize(values):
    centered = values - jnp.mean(values, axis=-1, keepdims=True)
    inverse = lax.rsqrt(jnp.mean(centered * centered, axis=-1, keepdims=True) + 1e-05)
    return centered * inverse, inverse


def norm_back(grad, hat, inverse, gain):
    scaled = grad * gain
    return inverse * (
        scaled
        - jnp.mean(scaled, axis=-1, keepdims=True)
        - hat * jnp.mean(scaled * hat, axis=-1, keepdims=True)
    )


def gauss_tail(u):
    size = jnp.abs(u)
    t = 1.0 / (1.0 + (0.3275911 * 0.7071067811865476) * size)
    bell = jnp.exp2(-0.7213475204444817 * (u * u))
    poly = 0.5 * 1.061405429 * t - 0.5 * 1.453152027
    poly = poly * t + 0.5 * 1.421413741
    poly = poly * t - 0.5 * 0.284496736
    poly = poly * t + 0.5 * 0.254829592
    return poly * t * bell, bell, size


def head_pair(block, low_lane):
    zero = jnp.zeros_like(block)
    return jnp.concatenate(
        [jnp.where(low_lane, block, zero), jnp.where(low_lane, zero, block)], axis=0
    )


def softmax_half(scores, bias):
    scores = scores + bias
    top = jnp.max(scores, axis=-1, keepdims=True)
    powers = jnp.exp(scores - top)
    return powers * (1.0 / jnp.sum(powers, axis=-1, keepdims=True))


def unit_rows(pooled):
    return pooled * lax.rsqrt(jnp.sum(pooled * pooled, axis=-1, keepdims=True) + 1e-06)


def mean_down(total, count, down):
    mean = total * (1.0 / count)
    high = mean.astype(BF)
    low = (mean - high.astype(F32)).astype(BF)
    both = dot(jnp.concatenate([high, low], axis=0), down)
    return both[: mean.shape[0]] + both[mean.shape[0] :]


def image_kernel(
    tok, wq_h, wo_h, wu_h, wd_h, vec, ub, out, wq, wo, wu, wd, x, h, qkv, att, act_sum, r1_sum, bias_row, stage, sem
):
    step, steps = pl.program_id(0), pl.num_programs(0)
    length, group, width = tok.shape
    rows = group * length
    hidden = wu.shape[1]
    copies = [
        pltpu.make_async_copy(src, dst, sem.at[i])
        for i, (src, dst) in enumerate(((wq_h, wq), (wo_h, wo), (wu_h, wu), (wd_h, wd)))
    ]

    @pl.when(step == 0)
    def _():
        for copy in copies:
            copy.start()

    def arrived(i):
        @pl.when(step == 0)
        def _():
            copies[i].wait()

    v = vec[...].astype(F32)
    bias_row[:, :width] = v[2:3]
    bias_row[:, width : 2 * width] = jnp.zeros((1, width), F32)
    bias_row[:, 2 * width :] = v[3:4]
    for k in range(width // 128):
        stage[k] = tok[:, :, k * 128 : (k + 1) * 128].astype(F32).reshape(rows, 128)
        for i in range(group):
            x[pl.ds(i * length, length), k * 128 : (k + 1) * 128] = stage[k, pl.ds(i, length, stride=group), :]

    def norm_rows(gain, shift):
        blk = 80

        def one(i):
            at = pl.ds(pl.multiple_of(i * blk, blk), blk)
            hat, _ = normalize(x[at, :])
            h[at, :] = (hat * gain + shift).astype(BF)

        repeat(rows // blk, one, 5)

    norm_rows(v[0:1], v[1:2])
    arrived(0)

    def project(i):
        at = pl.ds(pl.multiple_of(i * 256, 256), 256)
        qkv[:, at] = (dot(h[...], wq[:, at]) + bias_row[:, at]).astype(BF)

    repeat(3 * width // 256, project, 3)

    wins = rows // (2 * length)
    q_len = 112
    low_lane = lax.broadcasted_iota(jnp.int32, (128, 128), 1) < HEAD_DIM
    cols = range(0, width, 128)

    def window(w):
        q_at = pl.multiple_of((2 * length * w) // 16 * 16, 16)
        k_at = pl.multiple_of(jnp.minimum(q_at, rows - 128), 16)
        lo, mid, hi = 2 * w * length, (2 * w + 1) * length, (2 * w + 2) * length
        qi = q_at + lax.broadcasted_iota(jnp.int32, (q_len, 128), 0)
        ki = k_at + lax.broadcasted_iota(jnp.int32, (q_len, 128), 1)
        first = (qi >= lo) & (qi < mid) & (ki >= lo) & (ki < mid)
        second = (qi >= mid) & (qi < hi) & (ki >= mid) & (ki < hi)
        bias = jnp.where(first | second, 0.0, -1e30)
        q_rows, k_rows = pl.ds(q_at, q_len), pl.ds(k_at, 128)
        q2 = [qkv[q_rows, c : c + 128] * 0.125 for c in cols]
        k2 = [head_pair(qkv[k_rows, width + c : width + c + 128], low_lane) for c in cols]
        v2 = [head_pair(qkv[k_rows, 2 * width + c : 2 * width + c + 128], low_lane) for c in cols]
        scores = [dot(q, k, 1, 1) for q, k in zip(q2, k2)]
        probs = [
            jnp.concatenate(
                [softmax_half(s[:, :128], bias).astype(BF), softmax_half(s[:, 128:], bias).astype(BF)],
                axis=1,
            )
            for s in scores
        ]
        mine = (q_at + lax.broadcasted_iota(jnp.int32, (16, 128), 0)) >= lo
        for c, p, values in zip(cols, probs, v2):
            mixed = dot(p, values)
            old = att[pl.ds(q_at, 16), c : c + 128].astype(F32)
            att[pl.ds(q_at, 16), c : c + 128] = jnp.where(mine, mixed[:16], old).astype(BF)
            att[pl.ds(q_at + 16, q_len - 16), c : c + 128] = mixed[16:].astype(BF)

    repeat(wins, window, 2)

    arrived(1)
    for c in range(0, width, 256):
        x[:, c : c + 256] = x[:, c : c + 256] + (dot(att[...], wo[:, c : c + 256]) + v[4:5, c : c + 256])
    norm_rows(v[5:6], v[6:7])

    def image_sums(values):
        sums = []
        for i in range(group):
            lo, hi = i * length, (i + 1) * length
            a, b = lo // 8 * 8, -(-hi // 8) * 8
            part = values[a:b]
            row = a + lax.broadcasted_iota(jnp.int32, (b - a, 1), 0)
            if lo % 8 or hi % 8:
                part = jnp.where((row >= lo) & (row < hi), part, 0.0)
            sums.append(jnp.sum(part, axis=0, keepdims=True))
        return jnp.concatenate(sums, axis=0)

    place = pl.ds(pl.multiple_of(step * group, group), group)
    for c in range(0, width, 256):
        r1_sum[place, c : c + 256] = image_sums(x[:, c : c + 256])
    arrived(2)

    def expand(i):
        at = pl.ds(pl.multiple_of(i * 256, 256), 256)
        u = dot(h[...], wu[:, at]) + ub[:, at].astype(F32)
        tail, _, size = gauss_tail(u)
        act_sum[place, at] = image_sums(jnp.maximum(u, 0.0) - size * tail)

    repeat(hidden // 256, expand, 3)
    arrived(3)

    @pl.when(step == steps - 1)
    def _():
        pooled = r1_sum[...] * (1.0 / length) + mean_down(act_sum[...], length, wd[...]) + v[7:8]
        out[...] = unit_rows(pooled).astype(BF)


def image_forward(tokens, wq, wo, wu, wd, vec, ub):
    pairs, length, width = tokens.shape
    hidden = wu.shape[1]
    group = 16
    rows = group * length
    return pl.pallas_call(
        image_kernel,
        name="image_forward",
        grid=(pairs // group,),
        in_specs=[
            pl.BlockSpec((length, group, width), lambda i: (0, i, 0)),
            ANY,
            ANY,
            ANY,
            ANY,
            pl.BlockSpec((8, width), lambda i: (0, 0)),
            pl.BlockSpec((1, hidden), lambda i: (0, 0)),
        ],
        out_specs=pl.BlockSpec((pairs, width), lambda i: (0, 0)),
        out_shape=jax.ShapeDtypeStruct((pairs, width), BF),
        scratch_shapes=[
            pltpu.VMEM((width, 3 * width), BF),
            pltpu.VMEM((width, width), BF),
            pltpu.VMEM((width, hidden), BF),
            pltpu.VMEM((hidden, width), BF),
            pltpu.VMEM((rows, width), F32),
            pltpu.VMEM((rows, width), BF),
            pltpu.VMEM((rows, 3 * width), BF),
            pltpu.VMEM((rows, width), BF),
            pltpu.VMEM((pairs, hidden), F32),
            pltpu.VMEM((pairs, width), F32),
            pltpu.VMEM((1, 3 * width), F32),
            pltpu.VMEM((width // 128, rows, 128), F32),
            pltpu.SemaphoreType.DMA((4,)),
        ],
        compiler_params=params(),
        cost_estimate=pl.CostEstimate(
            flops=2 * pairs * length * width * (4 * width + hidden),
            bytes_accessed=2 * (4 * width * width + 2 * width * hidden + pairs * length * width),
            transcendentals=pairs * length * hidden,
        ),
    )(jnp.swapaxes(tokens, 0, 1), wq, wo, wu, wd, vec, ub.reshape(1, hidden))


def pack_rows(width, hidden):
    piece, rows = width // PX, width // PF
    return piece, rows, hidden // PF


def weight_copies(packed, which, dst, sem, base, width, hidden):
    piece, rows, frows = pack_rows(width, hidden)
    q_pieces, u_pieces = 3, hidden // width
    spans = {
        "qkv": (0, q_pieces, rows),
        "out": (q_pieces * rows, 1, rows),
        "up": ((q_pieces + 1) * rows, u_pieces, rows),
        "down": ((q_pieces + 1 + u_pieces) * rows, 1, frows),
    }
    start, count, tall = spans[which]
    copies = []
    for x in range(PX):
        for p in range(count):
            copies.append(
                pltpu.make_async_copy(
                    packed.at[pl.ds(x * PF, PF), pl.ds(start + p * tall, tall), :],
                    dst.at[:, :, pl.ds((x * count + p) * piece, piece)],
                    sem.at[base + len(copies)],
                )
            )
    return copies


def natural(ref):
    blocks, rows, cols = ref.shape
    return ref[...].reshape(blocks * rows, cols)


def weight_scratch(which, width, hidden):
    rows, frows = width // PF, hidden // PF
    shape = {
        "qkv": (PF, rows, 3 * width),
        "out": (PF, rows, width),
        "up": (PF, rows, hidden),
        "down": (PF, frows, width),
    }[which]
    return pltpu.VMEM(shape, BF)


def contrast(low, images, live, same, groups, own, own_group, power, row_part, col_sum, loss_part):
    scores = LOGIT_SCALE * dot(low, images[...], 1, 1)
    exps = jnp.exp(scores)
    live_own, same_own = own[:, 0:1], own[:, 1:2]
    power[...] = exps
    rows = jnp.sum(exps * live_own, axis=0, keepdims=True)
    tiled = jnp.concatenate(
        [rows[:, k * 128 : (k + 1) * 128] for k in range(rows.shape[1] // 128)], axis=0
    )
    for d in range(row_part.shape[0]):
        row_part[d] = tiled
    cols = jnp.sum(exps * live[...], axis=1, keepdims=True)
    col_sum[...] = cols
    pair = jnp.where(own_group[...] == groups[...], live_own * live[...], 0.0)
    linear = pair * scores * (1.0 / same_own + 1.0 / same[...])
    losses = live_own * jnp.log(cols) - jnp.sum(linear, axis=1, keepdims=True)
    loss_part[...] = jnp.broadcast_to(jnp.sum(losses, axis=0, keepdims=True), loss_part.shape)


def text_mask(size, length):
    row = lax.broadcasted_iota(jnp.int32, (size, size), 0) // length
    col = lax.broadcasted_iota(jnp.int32, (size, size), 1) // length
    return jnp.where(row == col, 0.0, -1e30)


def text_forward_kernel(
    length, tok, packed, vec, ub, images_i, live, same, groups, own, own_group,
    h1_o, qkv_o, att_o, r1_o, h2_o, slope_o, acts, pooled_out, power, row_part, col_sum, loss_part,
    wq, wo, wu, wd, total, bias_row, h1, qkv, att, r1, h2, slope, sem, images, out_sem
):
    rows, width = tok.shape
    hidden = slope.shape[1]
    texts = rows // length
    load = {}
    base = 0
    for which, dst in (("qkv", wq), ("out", wo), ("up", wu), ("down", wd)):
        load[which] = weight_copies(packed, which, dst, sem, base, width, hidden)
        base += len(load[which])
        for copy in load[which]:
            copy.start()
    v = vec[...].astype(F32)
    bias_row[:, :width] = v[2:3]
    bias_row[:, width : 2 * width] = jnp.zeros((1, width), F32)
    bias_row[:, 2 * width :] = v[3:4]
    blk = 128

    def norm_rows(src, dst, gain, shift):
        def one(i):
            at = pl.ds(pl.multiple_of(i * blk, blk), blk)
            hat, _ = normalize(src[at, :].astype(F32))
            dst[at, :] = (hat * gain + shift).astype(BF)

        repeat(rows // blk, one, 2)

    norm_rows(tok, h1, v[0:1], v[1:2])
    saves = move([(h1, h1_o)], out_sem)
    (gathered,) = move([(images_i, images)], out_sem, 6)
    for copy in load["qkv"]:
        copy.wait()

    def project(i):
        at = pl.ds(pl.multiple_of(i * 256, 256), 256)
        qkv[:, at] = (dot(h1[...], wq[:, :, at].reshape(width, 256)) + bias_row[:, at]).astype(BF)

    repeat(3 * width // 256, project, 3)
    saves += move([(qkv, qkv_o)], out_sem, 1)
    low_lane = lax.broadcasted_iota(jnp.int32, (blk, 128), 1) < HEAD_DIM
    bias = text_mask(blk, length)
    cols = range(0, width, 128)

    def attend(i):
        at = pl.ds(pl.multiple_of(i * blk, blk), blk)
        q2 = [qkv[at, c : c + 128] * 0.125 for c in cols]
        k2 = [head_pair(qkv[at, width + c : width + c + 128], low_lane) for c in cols]
        v2 = [head_pair(qkv[at, 2 * width + c : 2 * width + c + 128], low_lane) for c in cols]
        scores = [dot(q, k, 1, 1) for q, k in zip(q2, k2)]
        probs = [
            jnp.concatenate(
                [softmax_half(s[:, :blk], bias).astype(BF), softmax_half(s[:, blk:], bias).astype(BF)],
                axis=1,
            )
            for s in scores
        ]
        for c, p, values in zip(cols, probs, v2):
            att[at, c : c + 128] = dot(p, values).astype(BF)

    repeat(rows // blk, attend, 2)
    saves += move([(att, att_o)], out_sem, 2)
    for copy in load["out"]:
        copy.wait()
    for c in range(0, width, 256):
        r1[:, c : c + 256] = tok[:, c : c + 256].astype(F32) + (
            dot(att[...], wo[:, :, c : c + 256].reshape(width, 256)) + v[4:5, c : c + 256]
        )
    saves += move([(r1, r1_o)], out_sem, 3)
    norm_rows(r1, h2, v[5:6], v[6:7])
    saves += move([(h2, h2_o)], out_sem, 4)
    for copy in load["up"]:
        copy.wait()

    def expand(i):
        at = pl.ds(pl.multiple_of(i * 256, 256), 256)
        u = dot(h2[...], wu[:, :, at].reshape(width, 256)) + ub[:, at].astype(F32)
        tail, bell, _ = gauss_tail(u)
        phi = jnp.where(u >= 0.0, 1.0 - tail, tail)
        act = u * phi
        slope[:, at] = (phi + u * (bell * 0.3989422804014327)).astype(BF)
        sums = jnp.sum(act.reshape(texts, length, 256), axis=1)
        total[:, at] = sums
        acts[:, at] = sums.astype(BF)

    repeat(hidden // 256, expand, 3)
    saves += move([(slope, slope_o)], out_sem, 5)
    for copy in load["down"]:
        copy.wait()
    mean_r1 = jnp.sum(r1[...].reshape(texts, length, width), axis=1) * (1.0 / length)
    pooled = mean_r1 + mean_down(total[...], length, natural(wd)) + v[7:8]
    pooled_out[...] = pooled
    gathered.wait()
    contrast(
        unit_rows(pooled).astype(BF), images, live, same, groups, own, own_group, power, row_part, col_sum, loss_part
    )
    for copy in saves:
        copy.wait()


def text_forward(
    tokens, packed, vec, ub, images, live, same, groups, own, own_group, length, hidden, copies_of
):
    rows, width = tokens.shape
    texts = rows // length
    pairs = images.shape[0]
    shape = jax.ShapeDtypeStruct
    copies = PX * (3 + 1 + hidden // width + 1)
    return pl.pallas_call(
        functools.partial(text_forward_kernel, length),
        name="text_forward",
        in_specs=[WHOLE, ANY, WHOLE, WHOLE, ANY] + [WHOLE] * 5,
        out_specs=[ANY] * 6 + [WHOLE] * 6,
        out_shape=[
            shape((rows, width), BF),
            shape((rows, 3 * width), BF),
            shape((rows, width), BF),
            shape((rows, width), F32),
            shape((rows, width), BF),
            shape((rows, hidden), BF),
            shape((texts, hidden), BF),
            shape((texts, width), F32),
            shape((texts, pairs), F32),
            shape((copies_of, pairs // 128, 128), F32),
            shape((texts, 1), F32),
            shape((8, 128), F32),
        ],
        scratch_shapes=[weight_scratch(w, width, hidden) for w in ("qkv", "out", "up", "down")]
        + [
            pltpu.VMEM((texts, hidden), F32),
            pltpu.VMEM((1, 3 * width), F32),
            pltpu.VMEM((rows, width), BF),
            pltpu.VMEM((rows, 3 * width), BF),
            pltpu.VMEM((rows, width), BF),
            pltpu.VMEM((rows, width), F32),
            pltpu.VMEM((rows, width), BF),
            pltpu.VMEM((rows, hidden), BF),
            pltpu.SemaphoreType.DMA((copies,)),
            pltpu.VMEM((pairs, width), BF),
            pltpu.SemaphoreType.DMA((7,)),
        ],
        compiler_params=params(),
        cost_estimate=pl.CostEstimate(
            flops=2 * rows * width * (4 * width + hidden),
            bytes_accessed=2 * (4 * width * width + 2 * width * hidden + 12 * rows * width),
            transcendentals=rows * hidden,
        ),
    )(tokens, packed, vec, ub, images, live, same, groups, own, own_group)


def relative_kernel(where, h1_i, h2_i, att_i, h1_o, h2_o, att_o, h1, h2, att, h1_t, h2_t, att_t, sem):
    width = h1.shape[1]
    block = width // PF
    my, mz, mc = where[1], where[2], where[3]
    loads = move([(h2_i, h2), (h1_i, h1), (att_i, att)], sem)
    saves = []
    for n, (src, dst, out) in enumerate(((h2, h2_t, h2_o), (h1, h1_t, h1_o), (att, att_t, att_o))):
        loads[n].wait()
        turned = src[...].T
        for z in range(4):
            for y in range(2):
                for c in range(2):
                    f = (z * 2 + y) * 2 + c
                    place = (((c ^ mc) * 2 + (y ^ my)) * 4 + (z ^ mz)) * block
                    dst[pl.ds(pl.multiple_of(place, block), block), :] = turned[
                        f * block : (f + 1) * block
                    ]
        saves += move([(dst, out)], sem, 3 + n)
    for copy in saves:
        copy.wait()


SMEM = pl.BlockSpec(memory_space=pltpu.SMEM)


def relative_rows(where, h1, h2, att):
    rows, width = h1.shape
    return pl.pallas_call(
        relative_kernel,
        name="relative_rows",
        in_specs=[SMEM, ANY, ANY, ANY],
        out_specs=[ANY] * 3,
        out_shape=[jax.ShapeDtypeStruct((width, rows), BF)] * 3,
        scratch_shapes=[pltpu.VMEM((rows, width), BF)] * 3
        + [pltpu.VMEM((width, rows), BF)] * 3
        + [pltpu.SemaphoreType.DMA((6,))],
        compiler_params=params(),
        cost_estimate=pl.CostEstimate(flops=0, bytes_accessed=12 * rows * width, transcendentals=0),
    )(where, h1, h2, att)


def grad_shapes(width):
    block, half = width // PF, width
    return [jax.ShapeDtypeStruct((2, 2, 4, block, half), BF)] * 4


def put_grad(values, outs, x_rel, at, second):
    width, cols = values.shape
    block = width // PF
    low = values.astype(BF)
    for c in range(2):
        for y in range(2):
            piece = low[(c * 2 + y) * 4 * block : (c * 2 + y + 1) * 4 * block].reshape(4, block, cols)
            if second:
                outs[2 + c, y, x_rel, :, :, pl.ds(at, cols)] = piece
            else:
                outs[c, x_rel, y, :, :, pl.ds(at, cols)] = piece


def start_grads(parts, outs, sem, x):
    return move(
        [(parts.at[n, x], outs[n].at[x]) for n in range(2)]
        + [(parts.at[n, :, x], outs[n].at[:, x]) for n in range(2, 4)],
        sem,
        4 * x,
    )


def back_one_kernel(
    length, shard,
    where, power, row_all, col_sum, images_i, live, same, groups, own, own_group, pooled, packed, vec,
    slope_i, h2_i, r1_i, acts,
    factors_o, keep_a, send_a, keep_b, send_b, bias_up, down_bias, dr1_o, dz_o, da_o, sums, loss_rows,
    factors, wd, wu, wo, dact, images, slope, h2_t, r1, du, dr1, dz_s, da_s, dy, parts, sem, in_sem, out_sem,
):
    rows, hidden = slope.shape
    texts = rows // length
    width = h2_t.shape[0]
    (gathered,) = move([(images_i, images)], in_sem)
    down = weight_copies(packed, "down", wd, sem, 0, width, hidden)
    up = weight_copies(packed, "up", wu, sem, len(down), width, hidden)
    out = weight_copies(packed, "out", wo, sem, len(down) + len(up), width, hidden)
    for copy in down:
        copy.start()
    saved = move([(slope_i, slope), (h2_i, h2_t)], in_sem, 1)
    for copy in up + out:
        copy.start()
    saved += move([(r1_i, r1)], in_sem, 3)
    totals = jnp.sum(row_all[...], axis=0)
    row_sum = jnp.concatenate([totals[k : k + 1] for k in range(totals.shape[0])], axis=1)
    live_own, same_own = own[:, 0:1], own[:, 1:2]
    factor = LOSS_WEIGHT / (2.0 * jnp.sum(live[...], axis=1, keepdims=True))
    pair = factor * live_own * live[...]
    match = jnp.where(own_group[...] == groups[...], 1.0 / same_own + 1.0 / same[...], 0.0)
    grad_scores = pair * (power[...] * (1.0 / row_sum + 1.0 / col_sum[...]) - match)
    gathered.wait()
    grad_low = LOGIT_SCALE * dot(grad_scores.astype(BF), images[...])
    pool = pooled[...]
    inverse = lax.rsqrt(jnp.sum(pool * pool, axis=-1, keepdims=True) + 1e-06)
    along = jnp.sum(pool * grad_low, axis=-1, keepdims=True)
    dy[...] = inverse * (grad_low - pool * (inverse * inverse * along)) * (1.0 / length)
    dm = dy[...].astype(BF)
    loss_rows[...] = jnp.broadcast_to(
        jnp.sum(live[...] * jnp.log(row_sum), axis=1, keepdims=True), loss_rows.shape
    )
    parts_x, parts_f = shard
    piece_x, piece_f = width // parts_x, hidden // parts_f
    for f in range(parts_f):
        left = acts[:, f * piece_f : (f + 1) * piece_f]
        for x in range(parts_x):
            factors[x * parts_f + f, :, piece_x:] = left
            factors[x * parts_f + f, :, :piece_x] = dm[:, x * piece_x : (x + 1) * piece_x]
    sent = move([(factors, factors_o)], out_sem, 11)
    down_bias[...] = length * jnp.sum(dm.astype(F32), axis=0, keepdims=True)
    for copy in down:
        copy.wait()
    dact[...] = dot(dm, natural(wd), 1, 1)
    saved[0].wait()

    saved[1].wait()
    half = hidden // PX
    outs = (keep_a, send_a, keep_b, send_b)
    for x in range(PX):
        first = (x ^ where[0]) * half

        def grads(i):
            c = pl.multiple_of(i * 256, 256)
            for second in range(2):
                at = pl.ds(pl.multiple_of(first + c + second * width, 256), 256)
                spread = jnp.broadcast_to(dact[:, at].reshape(texts, 1, 256), (texts, length, 256))
                part = (spread.reshape(rows, 256) * slope[:, at].astype(F32)).astype(BF)
                du[:, at] = part
                bias_up[:, at] = jnp.sum(part.astype(F32), axis=0, keepdims=True)
                put_grad(dot(h2_t[...], part), parts, x, c, second)

        repeat(width // 256, grads, 3)
        sent += start_grads(parts, outs, out_sem, x)

    v = vec[...].astype(F32)
    blk = 128
    for copy in up:
        copy.wait()

    def product(i):
        at = pl.ds(pl.multiple_of(i * (rows // 2), rows // 2), rows // 2)
        dr1[at, :] = dot(du[at, :], natural(wu), 1, 1)

    repeat(2, product)
    sums[...] = jnp.zeros((8, width), F32)
    some = blk // length
    saved[2].wait()

    def back(i):
        at = pl.ds(pl.multiple_of(i * blk, blk), blk)
        hat, inverse = normalize(r1[at, :])
        grad = dr1[at, :]
        sums[1:2, :] += jnp.sum(grad * hat, axis=0, keepdims=True)
        sums[2:3, :] += jnp.sum(grad, axis=0, keepdims=True)
        spread = jnp.broadcast_to(
            dy[pl.ds(pl.multiple_of(i * some, some), some), :].reshape(some, 1, width), (some, length, width)
        ).reshape(blk, width)
        grad = spread + norm_back(grad, hat, inverse, v[5:6])
        dr1[at, :] = grad
        low = grad.astype(BF)
        dz_s[at, :] = low
        sums[0:1, :] += jnp.sum(low.astype(F32), axis=0, keepdims=True)

    repeat(rows // blk, back)
    sent += move([(dr1, dr1_o), (dz_s, dz_o)], out_sem, 8)
    for copy in out:
        copy.wait()
    da_s[...] = dot(dz_s[...], natural(wo), 1, 1).astype(BF)
    sent += move([(da_s, da_o)], out_sem, 10)
    for copy in sent:
        copy.wait()


def back_one(
    where, power, row_all, col_sum, images, live, same, groups, own, own_group, pooled, packed, vec, slope,
    h2_t, r1, acts, length, shard,
):
    rows, hidden = slope.shape
    width = h2_t.shape[0]
    texts = rows // length
    payload = (shard[0] * shard[1], texts, width // shard[0] + hidden // shard[1])
    shape = jax.ShapeDtypeStruct
    return pl.pallas_call(
        functools.partial(back_one_kernel, length, shard),
        name="back_one",
        in_specs=[SMEM] + [WHOLE] * 3 + [ANY] + [WHOLE] * 6 + [ANY, WHOLE, ANY, ANY, ANY, WHOLE],
        out_specs=[ANY] * 5 + [WHOLE] * 2 + [ANY] * 3 + [WHOLE] * 2,
        out_shape=[
            shape(payload, BF),
            *grad_shapes(width),
            shape((1, hidden), F32),
            shape((1, width), F32),
            shape((rows, width), F32),
            shape((rows, width), BF),
            shape((rows, width), BF),
            shape((8, width), F32),
            shape((8, 128), F32),
        ],
        scratch_shapes=[
            pltpu.VMEM(payload, BF),
            weight_scratch("down", width, hidden),
            weight_scratch("up", width, hidden),
            weight_scratch("out", width, hidden),
            pltpu.VMEM((texts, hidden), F32),
            pltpu.VMEM(images.shape, BF),
            pltpu.VMEM((rows, hidden), BF),
            pltpu.VMEM((width, rows), BF),
            pltpu.VMEM((rows, width), F32),
            pltpu.VMEM((rows, hidden), BF),
            pltpu.VMEM((rows, width), F32),
            pltpu.VMEM((rows, width), BF),
            pltpu.VMEM((rows, width), BF),
            pltpu.VMEM((texts, width), F32),
            pltpu.VMEM((4,) + grad_shapes(width)[0].shape, BF),
            pltpu.SemaphoreType.DMA((PX * (2 + hidden // width),)),
            pltpu.SemaphoreType.DMA((4,)),
            pltpu.SemaphoreType.DMA((12,)),
        ],
        compiler_params=params(),
        cost_estimate=pl.CostEstimate(
            flops=2 * rows * width * (2 * hidden + width), bytes_accessed=16 * width * hidden, transcendentals=0
        ),
    )(
        where, power, row_all, col_sum, images, live, same, groups, own, own_group, pooled, packed, vec,
        slope, h2_t, r1, acts,
    )


def back_two_kernel(
    length, where, qkv_i, da_i, dz_i, h1_i, att_i, up_a, up_a_new, up_b, up_b_new,
    dqkv_o, keep_a, send_a, keep_b, send_b, up_a_keep, up_a_send, up_b_keep, up_b_send, sums,
    qkv, da_s, dz, h1_t, att_t, dqkv, parts, held, come, sem, out_sem, up_sem,
):
    rows, width = da_s.shape
    blk = 128
    loads = move([(qkv_i, qkv), (da_i, da_s), (att_i, att_t), (dz_i, dz), (h1_i, h1_t)], sem)
    arrivals = move(
        [(up_a, held.at[0]), (up_a_new, come.at[0]), (up_b, held.at[1]), (up_b_new, come.at[1])], up_sem
    )
    for copy in loads[:2]:
        copy.wait()
    low_lane = lax.broadcasted_iota(jnp.int32, (blk, 128), 1) < HEAD_DIM
    bias = text_mask(blk, length)
    cols = range(0, width, 128)
    def group(i):
        at = pl.ds(pl.multiple_of(i * blk, blk), blk)
        take = lambda base, c: qkv[at, base + c : base + c + 128]
        q2 = [take(0, c) * 0.125 for c in cols]
        k2 = [head_pair(take(width, c), low_lane) for c in cols]
        v2 = [head_pair(take(2 * width, c), low_lane) for c in cols]
        da = [da_s[at, c : c + 128] for c in cols]
        scores = [dot(k, q, 1, 1) for k, q in zip(k2, q2)]
        grads = [dot(v, d, 1, 1) for v, d in zip(v2, da)]
        probs, deltas = [], []
        for score, grad in zip(scores, grads):
            p_low, d_low = [], []
            for half in range(2):
                s = score[half * blk : (half + 1) * blk] + bias
                g = grad[half * blk : (half + 1) * blk]
                powers = jnp.exp(s - jnp.max(s, axis=0, keepdims=True))
                soft = powers * (1.0 / jnp.sum(powers, axis=0, keepdims=True))
                p_low.append(soft.astype(BF))
                d_low.append((soft * (g - jnp.sum(g * soft, axis=0, keepdims=True))).astype(BF))
            probs.append(jnp.concatenate(p_low, axis=0))
            deltas.append(jnp.concatenate(d_low, axis=0))
        for n, c in enumerate(cols):
            dq = dot(deltas[n], k2[n], 0, 0) * 0.125
            dk = dot(deltas[n], q2[n])
            dv = dot(probs[n], da[n])
            dqkv[at, c : c + 128] = dq.astype(BF)
            dqkv[at, width + c : width + c + 128] = jnp.where(
                low_lane, dk[:blk], dk[blk:]
            ).astype(BF)
            dqkv[at, 2 * width + c : 2 * width + c + 128] = jnp.where(
                low_lane, dv[:blk], dv[blk:]
            ).astype(BF)

    repeat(rows // blk, group, 2)
    sums[0:1, :] = jnp.sum(dqkv[:, :width].astype(F32), axis=0, keepdims=True)
    sums[1:2, :] = jnp.sum(dqkv[:, 2 * width :].astype(F32), axis=0, keepdims=True)
    sums[2:8, :] = jnp.zeros((6, width), F32)
    sent = move([(dqkv, dqkv_o)], out_sem, 8)
    for copy in arrivals:
        copy.wait()

    def add(i):
        n, first, second = i // 4, i // 2 % 2, i % 2
        held[n, first, second] = (
            held[n, first, second].astype(F32) + come[n, first, second].astype(F32)
        ).astype(BF)

    repeat(8, add)
    sent += move(
        [
            (held.at[0, 0], up_a_keep),
            (held.at[0, 1], up_a_send),
            (held.at[1, 0], up_b_keep),
            (held.at[1, 1], up_b_send),
        ],
        up_sem,
        4,
    )
    for copy in loads[2:]:
        copy.wait()
    piece = width // PX
    outs = (keep_a, send_a, keep_b, send_b)
    for x in range(PX):
        other = x ^ where[0]
        first = other * (3 * piece)

        def chunk(i):
            c = pl.multiple_of(i * 256, 256)
            part = dqkv[:, pl.ds(pl.multiple_of(first + c, 128), 256)]
            put_grad(dot(h1_t[...], part), parts, x, c, 0)

        repeat(width // 256, chunk, 3)
        part = dqkv[:, pl.ds(pl.multiple_of(first + width, 128), piece)]
        put_grad(dot(h1_t[...], part), parts, x, 0, 1)
        part = dz[:, pl.ds(pl.multiple_of(other * piece, 128), piece)]
        put_grad(dot(att_t[...], part), parts, x, piece, 1)
        sent += start_grads(parts, outs, out_sem, x)
    for copy in sent:
        copy.wait()


def back_two(where, qkv, da, dz, h1_t, att_t, up_parts, length):
    rows, width = da.shape
    shape = jax.ShapeDtypeStruct
    whole = grad_shapes(width)
    return pl.pallas_call(
        functools.partial(back_two_kernel, length),
        name="back_two",
        in_specs=[SMEM] + [ANY] * 9,
        out_specs=[ANY] * 9 + [WHOLE],
        out_shape=[shape((rows, 3 * width), BF), *whole, *[shape(whole[0].shape[1:], BF)] * 4, shape((8, width), F32)],
        scratch_shapes=[
            pltpu.VMEM((rows, 3 * width), BF),
            pltpu.VMEM((rows, width), BF),
            pltpu.VMEM((rows, width), BF),
            pltpu.VMEM((width, rows), BF),
            pltpu.VMEM((width, rows), BF),
            pltpu.VMEM((rows, 3 * width), BF),
            pltpu.VMEM((4,) + whole[0].shape, BF),
            pltpu.VMEM((2,) + whole[0].shape, BF),
            pltpu.VMEM((2,) + whole[0].shape, BF),
            pltpu.SemaphoreType.DMA((5,)),
            pltpu.SemaphoreType.DMA((9,)),
            pltpu.SemaphoreType.DMA((8,)),
        ],
        compiler_params=params(),
        cost_estimate=pl.CostEstimate(
            flops=2 * rows * width * (1280 + 4 * width), bytes_accessed=20 * rows * width, transcendentals=rows * width
        ),
    )(where, qkv, da, dz, h1_t, att_t, *up_parts)


def back_third_kernel(
    parts_f, dr1_i, dqkv_i, tok_i, packed, vec, sums, bias_sums, down_bias, bias_up, loss_part, dx_o, share, all_sums, wq, dr1, tok, dx, sem, dqkv, own_sem
):
    rows, width = tok.shape
    loads = weight_copies(packed, "qkv", wq, sem, 0, width, width)
    for copy in loads:
        copy.start()
    saved = move([(dqkv_i, dqkv), (dr1_i, dr1), (tok_i, tok)], own_sem)
    saved[0].wait()
    v = vec[...].astype(F32)
    for copy in loads:
        copy.wait()
    half = rows // 2

    def product(i):
        at = pl.ds(pl.multiple_of(i * half, half), half)
        dx[at, :] = dot(dqkv[at, :], natural(wq), 1, 1)

    repeat(2, product)
    for copy in saved[1:]:
        copy.wait()
    all_sums[0:2, :] = jnp.zeros((2, width), F32)
    blk = 128

    def back(i):
        at = pl.ds(pl.multiple_of(i * blk, blk), blk)
        hat, inverse = normalize(tok[at, :].astype(F32))
        grad = dx[at, :]
        all_sums[0:1, :] += jnp.sum(grad * hat, axis=0, keepdims=True)
        all_sums[1:2, :] += jnp.sum(grad, axis=0, keepdims=True)
        dx[at, :] = dr1[at, :] + norm_back(grad, hat, inverse, v[0:1])

    repeat(rows // blk, back)
    (save,) = move([(dx, dx_o)], own_sem, 3)
    all_sums[2:4, :] = bias_sums[0:2, :]
    all_sums[4:7, :] = sums[0:3, :]
    all_sums[7:8, :] = down_bias[...]
    every = all_sums[...]
    piece, tall = width // parts_f, bias_up.shape[1] // parts_f
    devices = share.shape[0]
    used = piece + tall // 8
    for f in range(parts_f):
        bias = bias_up[:, f * tall : (f + 1) * tall]
        bias = jnp.concatenate([bias[:, r * tall // 8 : (r + 1) * tall // 8] for r in range(8)], axis=0)
        block = jnp.concatenate(
            [every[:, f * piece : (f + 1) * piece], bias, loss_part[:, : 128 - used]], axis=1
        )
        for x in range(devices // parts_f):
            share[x * parts_f + f] = block
    save.wait()


def back_third(dr1, dqkv, tok, packed, vec, sums, bias_sums, down_bias, bias_up, loss_part, shard):
    rows, width = tok.shape
    shape = jax.ShapeDtypeStruct
    return pl.pallas_call(
        functools.partial(back_third_kernel, shard[1]),
        name="back_third",
        in_specs=[ANY, ANY, ANY, ANY] + [WHOLE] * 6,
        out_specs=[ANY, WHOLE],
        out_shape=[shape((rows, width), F32), shape((shard[0] * shard[1], 8, 128), F32)],
        scratch_shapes=[
            pltpu.VMEM((8, width), F32),
            weight_scratch("qkv", width, width),
            pltpu.VMEM((rows, width), F32),
            pltpu.VMEM((rows, width), BF),
            pltpu.VMEM((rows, width), F32),
            pltpu.SemaphoreType.DMA((PX * 3,)),
            pltpu.VMEM((rows, 3 * width), BF),
            pltpu.SemaphoreType.DMA((4,)),
        ],
        compiler_params=params(),
        cost_estimate=pl.CostEstimate(
            flops=6 * rows * width * width, bytes_accessed=14 * width * width, transcendentals=0
        ),
    )(dr1, dqkv, tok, packed, vec, sums, bias_sums, down_bias, bias_up, loss_part)


def fold_kernel(a_own, a_new, b_own, b_new, a_keep, a_send, b_keep, b_send):
    for own, new, keep, send in ((a_own, a_new, a_keep, a_send), (b_own, b_new, b_keep, b_send)):
        total = own[...].astype(F32) + new[...].astype(F32)
        keep[...] = total[0].astype(BF)
        send[...] = total[1].astype(BF)


def fold(a_own, a_new, b_own, b_new):
    shape = a_own.shape
    rest = 1
    for n in shape[1:-2]:
        rest *= n
    rows, cols = shape[-2:]
    view = lambda a: a.reshape(2, rest, rows, cols)
    steps = 2 if rest > 4 else 1
    pair = pl.BlockSpec((2, rest // steps, rows, cols), lambda i: (0, i, 0, 0))
    one = pl.BlockSpec((rest // steps, rows, cols), lambda i: (i, 0, 0))
    outs = pl.pallas_call(
        fold_kernel,
        name="fold",
        grid=(steps,),
        in_specs=[pair] * 4,
        out_specs=[one] * 4,
        out_shape=[jax.ShapeDtypeStruct((rest, rows, cols), BF)] * 4,
        compiler_params=params(18),
        cost_estimate=pl.CostEstimate(
            flops=4 * rest * rows * cols, bytes_accessed=24 * rest * rows * cols, transcendentals=0
        ),
    )(*(view(a) for a in (a_own, a_new, b_own, b_new)))
    return [o.reshape(shape[1:]) for o in outs]


def join_kernel(a_own, a_new, b_own, b_new, keep, send):
    half = a_own.shape[-1]
    for at, own, new in ((0, a_own, a_new), (half, b_own, b_new)):
        total = own[...].astype(F32) + new[...].astype(F32)
        for k in range(2):
            keep[k, :, at : at + half] = total[2 * k]
            send[k, :, at : at + half] = total[2 * k + 1].astype(BF)


def join(a_own, a_new, b_own, b_new):
    blocks, rows, cols = a_own.shape
    shape = jax.ShapeDtypeStruct
    return pl.pallas_call(
        join_kernel,
        name="join",
        in_specs=[WHOLE] * 4,
        out_specs=[WHOLE] * 2,
        out_shape=[shape((2, rows, 2 * cols), F32), shape((2, rows, 2 * cols), BF)],
        compiler_params=params(6),
        cost_estimate=pl.CostEstimate(
            flops=16 * rows * cols, bytes_accessed=40 * rows * cols, transcendentals=0
        ),
    )(a_own, a_new, b_own, b_new)


def turn_kernel(keep, new, stay, send):
    stay[...] = keep[0] + new[0].astype(F32)
    send[...] = (keep[1] + new[1].astype(F32)).astype(BF)


def turn(keep, new):
    blocks, rows, cols = keep.shape
    shape = jax.ShapeDtypeStruct
    return pl.pallas_call(
        turn_kernel,
        name="turn",
        in_specs=[WHOLE] * 2,
        out_specs=[WHOLE] * 2,
        out_shape=[shape((rows, cols), F32), shape((rows, cols), BF)],
        compiler_params=params(6),
        cost_estimate=pl.CostEstimate(
            flops=4 * rows * cols, bytes_accessed=18 * rows * cols, transcendentals=0
        ),
    )(keep, new)


def shifted(x, y, z, core):
    change = x * 16 + z * 4 + y * 2 + core
    return [(i, i ^ change) for i in range(32)]


def hop(array, x=0, y=0, z=0, core=0):
    return lax.ppermute(array, AXES, shifted(x, y, z, core))


def after(values, *others):
    return lax.optimization_barrier((tuple(values), others))[0]


def core_step(parts, *wait):
    keep_a, send_a, keep_b, send_b = parts
    new_a, new_b = hop(send_a, core=1), hop(send_b, core=1)
    keep_a, keep_b = after((keep_a, keep_b), *wait)
    return fold(keep_a, new_a, keep_b, new_b)


def first_step(parts, *wait):
    keep_a, send_a, keep_b, send_b = parts
    new_a, new_b = hop(send_a, x=1), hop(send_b, y=1)
    keep_a, keep_b = after((keep_a, keep_b), *wait)
    return fold(keep_a, new_a, keep_b, new_b)


def second_step(parts, *wait):
    keep_a, send_a, keep_b, send_b = parts
    new_a, new_b = hop(send_a, y=1), hop(send_b, x=1)
    keep_a, keep_b = after((keep_a, keep_b), *wait)
    return join(keep_a, new_a, keep_b, new_b)


def total_kernel(stay, new, *outs):
    total = stay[...] + new[...].astype(F32)
    at = 0
    for out in outs:
        out[...] = total[:, at : at + out.shape[1]]
        at += out.shape[1]


def third_step(parts, *wait):
    keep, send = parts
    new = hop(send, z=1)
    (keep,) = after((keep,), *wait)
    return turn(keep, new)


def last_step(parts, splits):
    stay, send = parts
    return pl.pallas_call(
        total_kernel,
        name="total",
        in_specs=[WHOLE] * 2,
        out_specs=[WHOLE] * len(splits),
        out_shape=[jax.ShapeDtypeStruct((stay.shape[0], n), F32) for n in splits],
        compiler_params=params(4),
    )(stay, hop(send, z=2))


def natural_grad(keep_a, send_a, keep_b, send_b):
    first = jnp.stack([keep_a, send_a])
    second = jnp.swapaxes(jnp.stack([keep_b, send_b]), 1, 2)
    whole = jnp.concatenate([first, second], axis=-1)
    core, x, y, z, rows, cols = whole.shape
    return whole.transpose(1, 3, 2, 0, 4, 5).reshape(x, z * y * core * rows, cols)


def pack_kernel(qkv, out, up, down, packed):
    rows, piece = out.shape
    at = 0
    for ref in (qkv, out, up, down):
        for c in range(0, ref.shape[1], piece):
            packed[at : at + ref.shape[0], :] = ref[:, c : c + piece]
            at += ref.shape[0]


def pack_block(qkv, out, up, down):
    piece = out.shape[1]
    total = sum(w.shape[0] * w.shape[1] for w in (qkv, out, up, down)) // piece
    return pl.pallas_call(
        pack_kernel,
        name="pack_block",
        in_specs=[WHOLE] * 4,
        out_specs=WHOLE,
        out_shape=jax.ShapeDtypeStruct((total, piece), BF),
        compiler_params=params(),
    )(qkv, out, up, down)


def gather_packed(qkv, out, up, down, dp, fsdp):
    if (dp, fsdp) == (PX, PF):
        return lax.all_gather(pack_block(qkv, out, up, down), AXES, axis=0)
    full = [
        lax.all_gather(lax.all_gather(w, "dp", axis=1, tiled=True), "fsdp", axis=0, tiled=True)
        for w in (qkv, out, up, down)
    ]
    blocks = []
    for x in range(PX):
        for f in range(PF):
            some = []
            for w in full:
                rows, cols = w.shape[0] // PF, w.shape[1] // PX
                some.append(w[f * rows : (f + 1) * rows, x * cols : (x + 1) * cols])
            blocks.append(pack_block(*some))
    return jnp.stack(blocks)


def scatter_columns(grad, dp, fsdp):
    parts, rows, cols = grad.shape
    if dp != parts:
        grad = jnp.swapaxes(grad, 0, 1).reshape(rows, dp, parts * cols // dp)
        grad = jnp.swapaxes(grad, 0, 1)
    return lax.psum_scatter(
        grad.reshape(dp * rows, -1), AXES, scatter_dimension=0, tiled=True
    ).astype(F32)


def body(
    image_tokens,
    text_tokens,
    image_qkv,
    image_out,
    image_up,
    image_down,
    image_vectors,
    image_up_bias,
    text_qkv,
    text_out,
    text_up,
    text_down,
    text_vectors,
    text_up_bias,
    pair_counts,
    pair_groups,
):
    dp, fsdp = lax.axis_size("dp"), lax.axis_size("fsdp")
    devices = dp * fsdp
    cap, length, width = text_tokens.shape
    hidden = image_up.shape[1]
    pairs = pair_groups.shape[0]
    me = lax.axis_index("dp") * fsdp + lax.axis_index("fsdp")

    grid_mesh = (dp, fsdp) == (PX, PF)
    packed = gather_packed(text_qkv, text_out, text_up, text_down, dp, fsdp)
    part = width // fsdp
    small = jnp.concatenate([text_vectors, text_up_bias.reshape(8, -1)], axis=1)
    if grid_mesh:
        small = jnp.broadcast_to(small[None], (fsdp,) + small.shape)
        small = lax.all_to_all(small, "fsdp", 0, 0, tiled=True)
    else:
        small = lax.all_gather(small, "fsdp", axis=0)
    vec = jnp.swapaxes(small[:, :, :part], 0, 1).reshape(8, width)
    ub = small[:, :, part:].reshape(1, hidden)
    bits = [lax.shift_right_logical(me, k) & 1 for k in range(5)]
    where = jnp.stack([bits[4], bits[1], 2 * bits[3] + bits[2], bits[0]])
    where = where if grid_mesh else jnp.zeros_like(where)

    image_low = image_forward(
        image_tokens, image_qkv, image_out, image_up, image_down, image_vectors, image_up_bias
    )
    if grid_mesh:
        images = image_low
        for change in (dict(z=1), dict(z=2), dict(x=1), dict(y=1), dict(core=1)):
            images = jnp.concatenate([images, hop(images, **change)], axis=0)
        far = jnp.arange(devices, dtype=jnp.int32) ^ me
        bit = lambda k: lax.shift_right_logical(far, k) & 1
        order = bit(2) + 2 * bit(3) + 4 * bit(4) + 8 * bit(1) + 16 * bit(0)
        images = jnp.take(images.reshape(devices, cap, width), order, axis=0).reshape(pairs, width)
    else:
        images = lax.all_gather(image_low, AXES, axis=0, tiled=True)

    slots = jnp.arange(cap, dtype=jnp.int32)
    live = (slots[None, :] < pair_counts[:, None]).reshape(pairs).astype(F32)
    same = jnp.maximum(
        jnp.sum(jnp.where(pair_groups[:, None] == pair_groups[None, :], live[None, :], 0.0), axis=1), 1.0
    )
    own_of = lambda array: lax.dynamic_slice_in_dim(array, me * cap, cap)
    own = jnp.stack([own_of(live), own_of(same)], axis=1)
    own_group = own_of(pair_groups).reshape(cap, 1)
    live_row, same_row, group_row = (a.reshape(1, pairs) for a in (live, same, pair_groups))
    live_total = jnp.sum(pair_counts).astype(F32)

    tokens = text_tokens.reshape(cap * length, width)
    h1, qkv, att, r1, h2, slope, acts, pooled, power, row_part, col_sum, loss_part = text_forward(
        tokens, packed, vec, ub, images, live_row, same_row, group_row, own, own_group, length, hidden,
        devices if grid_mesh else 1,
    )
    if grid_mesh:
        row_all = lax.all_to_all(row_part, AXES, 0, 0, tiled=True)
    else:
        row_all = lax.psum(row_part, AXES)
    h1_t, h2_t, att_t = relative_rows(where, h1, h2, att)
    factors, *up_parts, bias_up, down_bias, dr1, dz, da, sums, loss_rows = back_one(
        where, power, row_all, col_sum, images, live_row, same_row, group_row, own, own_group, pooled,
        packed, vec, slope, h2_t, r1, acts, length, (dp, fsdp),
    )
    keep_a, send_a, keep_b, send_b = up_parts
    if grid_mesh:
        travel = (keep_a, hop(send_a, core=1), keep_b, hop(send_b, core=1))
    else:
        travel = (keep_a, send_a, keep_b, send_b)
    dqkv, *both_parts, bias_sums = back_two(where, qkv, da, dz, h1_t, att_t, travel, length)
    att_parts = both_parts[:4]

    both = lax.all_to_all(factors, AXES, 0, 0, tiled=True).reshape(pairs, width // dp + hidden // fsdp)
    grad_down = dot(both[:, width // dp :], both[:, : width // dp], 0, 0)

    if grid_mesh:
        up_parts = both_parts[4:]
        att_parts = core_step(att_parts)
        (dqkv,) = after((dqkv,), *att_parts)
        dx, share = back_third(
            dr1, dqkv, tokens, packed, vec, sums, bias_sums, down_bias, bias_up, loss_part, (dp, fsdp)
        )
        up_parts = first_step(up_parts, dx)
        att_parts = first_step(att_parts, grad_down, *up_parts)
        up_parts = second_step(up_parts, *att_parts)
        (share,) = after((share,), *att_parts)
        att_parts = second_step(att_parts, *up_parts)
        up_parts = third_step(up_parts, *att_parts)
        att_parts = third_step(att_parts, *up_parts)
        (grad_up,) = last_step(up_parts, (hidden // dp,))
        grad_qkv, grad_out = last_step(att_parts, (3 * width // dp, width // dp))
    else:
        dx, share = back_third(
            dr1, dqkv, tokens, packed, vec, sums, bias_sums, down_bias, bias_up, loss_part, (dp, fsdp)
        )
        grad_attn = natural_grad(*att_parts)
        grad_up = scatter_columns(natural_grad(*up_parts), dp, fsdp)
        grad_qkv = scatter_columns(grad_attn[:, :, : 3 * width // PX], dp, fsdp)
        grad_out = scatter_columns(grad_attn[:, :, 3 * width // PX :], dp, fsdp)

    share = jnp.sum(lax.all_to_all(share, AXES, 0, 0, tiled=True), axis=0)
    grad_vec = share[:, :part]
    tall = hidden // fsdp // 8
    grad_bias = share[:, part : part + tall].reshape(hidden // fsdp)
    loss = (share[0, part + tall] + loss_rows[0, 0]) / (2.0 * live_total)

    return (
        loss,
        dx.reshape(text_tokens.shape),
        grad_qkv,
        grad_out,
        grad_up,
        grad_down,
        grad_vec,
        grad_bias,
    )


def solution(mesh):
    return jax.shard_map(
        body,
        mesh=mesh,
        in_specs=(
            P(AXES, None, None),
            P(AXES, None, None),
            P(),
            P(),
            P(),
            P(),
            P(),
            P(),
            P("fsdp", "dp"),
            P("fsdp", "dp"),
            P("fsdp", "dp"),
            P("fsdp", "dp"),
            P(None, "fsdp"),
            P("fsdp"),
            P(),
            P(),
        ),
        out_specs=(
            P(),
            P(AXES, None, None),
            P("fsdp", "dp"),
            P("fsdp", "dp"),
            P("fsdp", "dp"),
            P("fsdp", "dp"),
            P(None, "fsdp"),
            P("fsdp"),
        ),
        check_vma=False,
    )
```

profile of v0, /device:TPU:0, one launch (start us, length us, event | category | flops | bytes accessed | tf_op | source)
XLA Modules:
  0.0 269.5 jit_solution(11578938416900809978)
XLA Ops:
  7.2 1.9 pack_block.1
  9.1 0.7 reshape.197
  9.8 0.8 pad_maximum_fusion.3
  11.2 7.4 %all-to-all-start = ((bf16[16,8,72]{2,1,0:T(8,128)(2,1)}), bf16[16,8,72]{2,1,0:T(8,128)(2,1)S(1)}, u32[]{:S(2)}, u32[]{:S(2)}) async-start(bf16[16,8,72]{2,1,0:T(8,128)(2,1)} %broadcast_in_dim.39), calls=%async_computation | async-start | bytes 65536 | tf_op jit(solution)/shard_map/all_to_all | solution.py:1154
  18.6 1.3 reshape.200.ub
  19.9 49.9 %image_forward.1 = bf16[32,768]{1,0:T(8,128)(2,1)} custom-call(bf16[50,32,768]{2,1,0:T(8,128)(2,1)} %bitcast.52, bf16[768,2304]{1,0:T(8,128)(2,1)} %wq_h.1, bf16[768,768]{1,0:T(8,128)(2,1)} %wo_h.1, bf16[768,3072]{1,0:T(8,128)(2,1)} %wu_h.1, bf16[3072,768]{1,0:T(8,128)(2,1)} %wd_h.1, bf16[8,768]{1,0:T(8,128)(2,1)} %vec.1, bf16[1,3072]{1,0:T(2,128)(2,1)} %reshape.200.ub), custom_call_target="tpu_custom_call" | custom-call | flops 15099494400 | bytes 16613376 | tf_op jit(solution)/shard_map/image_forward/pallas_call | solution.py:229
  69.8 2.0 collective-permute-start
  72.5 4.6 %collective-permute-done = bf16[32,768]{1,0:T(8,128)(2,1)S(1)} collective-permute-done((bf16[32,768]{1,0:T(8,128)(2,1)}, bf16[32,768]{1,0:T(8,128)(2,1)S(1)}, u32[]{:S(2)}, u32[]{:S(2)}) %collective-permute-start) | collective-permute-done | bytes 49184 | tf_op jit(solution)/shard_map/ppermute | solution.py:1010
  77.1 0.8 pad_maximum_fusion.2
  77.9 2.1 collective-permute-start.1
  80.0 1.4 constant_dynamic-update-slice_fusion.4
  81.4 11.6 %collective-permute-done.1 = bf16[64,768]{1,0:T(8,128)(2,1)S(1)} collective-permute-done((bf16[64,768]{1,0:T(8,128)(2,1)S(1)}, bf16[64,768]{1,0:T(8,128)(2,1)S(1)}, u32[]{:S(2)}, u32[]{:S(2)}) %collective-permute-start.1) | collective-permute-done | bytes 98336 | tf_op jit(solution)/shard_map/ppermute | solution.py:1010
  93.0 0.8 pad_maximum_fusion.1
  93.8 1.5 collective-permute-start.2
  95.3 7.0 %collective-permute-done.2 = bf16[128,768]{1,0:T(8,128)(2,1)S(1)} collective-permute-done((bf16[128,768]{1,0:T(8,128)(2,1)S(1)}, bf16[128,768]{1,0:T(8,128)(2,1)S(1)}, u32[]{:S(2)}, u32[]{:S(2)}) %collective-permute-start.2) | collective-permute-done | bytes 196640 | tf_op jit(solution)/shard_map/ppermute | solution.py:1010
  102.3 0.8 pad_maximum_fusion
  103.1 1.5 collective-permute-start.3
  105.9 0.7 constant_dynamic-update-slice_fusion.1
  106.6 6.7 %collective-permute-done.3 = bf16[256,768]{1,0:T(8,128)(2,1)S(1)} collective-permute-done((bf16[256,768]{1,0:T(8,128)(2,1)S(1)}, bf16[256,768]{1,0:T(8,128)(2,1)S(1)}, u32[]{:S(2)}, u32[]{:S(2)}) %collective-permute-start.3) | collective-permute-done | bytes 393248 | tf_op jit(solution)/shard_map/ppermute | solution.py:1010
  113.3 0.8 constant_dynamic-update-slice_fusion
  115.1 0.7 copy.36.own_group
  115.8 0.7 copy.35.own
  116.6 0.7 reshape.199.ub
  117.3 0.7 reshape.198.vec
  118.8 1.4 bitcast_select_fusion.images_i
  120.2 22.3 %text_forward.1 = (bf16[512,768]{1,0:T(8,128)(2,1)}, bf16[512,2304]{1,0:T(8,128)(2,1)}, bf16[512,768]{1,0:T(8,128)(2,1)}, f32[512,768]{1,0:T(8,128)}, bf16[512,7...) custom-call(bf16[512,768]{1,0:T(8,128)(2,1)} %bitcast.45, ...), custom_call_target="tpu_custom_call" | custom-call | flops 4831838208 | bytes 23592960 | tf_op jit(solution)/shard_map/text_forward/pallas_call | solution.py:446
  142.5 5.2 %all-to-all-start.1 = ((f32[32,8,128]{2,1,0:T(8,128)}), f32[32,8,128]{2,1,0:T(8,128)S(1)}, u32[]{:S(2)}, u32[]{:S(2)}) async-start(f32[32,8,128]{2,1,0:T(8,128)} %get-tuple-element.84), calls=%async_computation.1 | async-start | bytes 262144 | tf_op jit(solution)/shard_map/all_to_all | solution.py:1194
  148.4 3.5 %relative_rows.1 = (bf16[768,512]{1,0:T(8,128)(2,1)}, bf16[768,512]{1,0:T(8,128)(2,1)}, bf16[768,512]{1,0:T(8,128)(2,1)}) custom-call(s32[4]{0:T(128)} %pad_add_fusion.where, bf16[512,768]{1,0:T(8,128)(2,1)} %get-tuple-element.88.h1_i, bf16[512,768]{1,0:T(8,128)(2,1)} %get-tuple-element.89.h2_i, bf16[512,768]{1,0:T(8,128)(2,1)} %get-tuple-element.90.att_i), custom_call_target="tpu_custom_call" | custom-call | bytes 4718592 | tf_op jit(solution)/shard_map/relative_rows/pallas_call | solution.py:515
  152.0 4.0 %all-to-all-done.1.row_all = f32[32,8,128]{2,1,0:T(8,128)S(1)} async-done(((f32[32,8,128]{2,1,0:T(8,128)}), f32[32,8,128]{2,1,0:T(8,128)S(1)}, u32[]{:S(2)}, u32[]{:S(2)}) %all-to-all-start.1) | async-done | bytes 131104 | tf_op jit(solution)/shard_map/all_to_all | solution.py:1194
  156.6 15.8 %back_one.1 = (bf16[32,32,576]{2,1,0:T(8,128)(2,1)}, bf16[2,2,4,48,768]{4,3,2,1,0:T(8,128)(2,1)}, bf16[2,2,4,48,768]{4,3,2,1,0:T(8,128)(2,1)}, bf16[2,2,4,48,768...) custom-call(s32[4]{0:T(128)} %pad_add_fusion.where, ...), custom_call_target="tpu_custom_call" | custom-call | flops 5435817984 | bytes 37748736 | tf_op jit(solution)/shard_map/back_one/pallas_call | solution.py:674
  173.0 2.9 %all-to-all-start.2 = ((bf16[32,32,576]{2,1,0:T(8,128)(2,1)}), bf16[32,32,576]{2,1,0:T(8,128)(2,1)S(1)}, u32[]{:S(2)}, u32[]{:S(2)}) async-start(bf16[32,32,576]{2,1,0:T(8,128)(2,1)} %get-tuple-element.122), calls=%async_computation.2 | async-start | bytes 2621440 | tf_op jit(solution)/shard_map/all_to_all | solution.py:1210
  175.9 1.5 collective-permute-done.6.up_b_new
  177.3 12.7 %back_two.1 = (bf16[512,2304]{1,0:T(8,128)(2,1)}, bf16[2,2,4,48,768]{4,3,2,1,0:T(8,128)(2,1)}, bf16[2,2,4,48,768]{4,3,2,1,0:T(8,128)(2,1)}, bf16[2,2,4,48,768]{4...) custom-call(s32[4]{0:T(128)} %pad_add_fusion.where, ...), custom_call_target="tpu_custom_call" | custom-call | flops 3422552064 | bytes 7864320 | tf_op jit(solution)/shard_map/back_two/pallas_call | solution.py:821
  190.6 0.8 collective-permute-start.9
  191.4 0.7 collective-permute-start.10
  192.1 1.1 collective-permute-done.7
  193.2 1.7 collective-permute-done.8
  194.8 1.3 copy-done
  196.1 1.3 copy-done.1
  197.4 1.6 fold.3
  199.0 0.8 copy-done.4
  199.8 0.8 collective-permute-start.11
  200.6 0.7 collective-permute-start.12
  201.3 7.2 %all-to-all-done.2 = bf16[32,32,576]{2,1,0:T(8,128)(2,1)S(1)} async-done(((bf16[32,32,576]{2,1,0:T(8,128)(2,1)}), bf16[32,32,576]{2,1,0:T(8,128)(2,1)S(1)}, u32[]{:S(2)}, u32[]{:S(2)}) %all-to-all-start.2) | async-done | bytes 1179680 | tf_op jit(solution)/shard_map/all_to_all | solution.py:1210
  208.5 1.1 fusion
  209.6 9.3 %back_third.1 = (f32[512,768]{1,0:T(8,128)}, f32[32,8,128]{2,1,0:T(8,128)}) custom-call(f32[512,768]{1,0:T(8,128)} %get-tuple-element.94.dr1_i, bf16[512,2304]{1,0:T(8,128)(2,1)} %get-tuple-element.115.dqkv_i, bf16[512,768]{1,0:T(8,128)(2,1)} %bitcast.46, bf16[32,576,384]{2,1,0:T(8,128)(2,1)} %bitcast.42, bf16[8,768]{1,0:T(8,128)(2,1)} %reshape.198.vec, ...), custom_call_target="tpu_custom_call" | custom-call | flops 1811939328 | bytes 8257536 | tf_op jit(solution)/shard_map/back_third/pallas_call | solution.py:903
  219.0 1.6 fold.4
  220.5 1.6 collective-permute-start.13
  222.7 1.5 collective-permute-done.12.b_new
  224.1 1.5 fold.5
  225.8 1.5 collective-permute-start.16
  227.2 3.3 %collective-permute-done.13.a_new = bf16[4,48,768]{2,1,0:T(8,128)(2,1)S(1)} collective-permute-done((bf16[4,48,768]{2,1,0:T(8,128)(2,1)S(1)}, bf16[4,48,768]{2,1,0:T(8,128)(2,1)S(1)}, u32[]{:S(2)}, u32[]{:S(2)}) %collective-permute-start.13) | collective-permute-done | bytes 294944 | tf_op jit(solution)/shard_map/ppermute | solution.py:1010
  230.9 1.4 collective-permute-start.17
  232.2 4.1 %collective-permute-done.15.a_new = bf16[4,48,768]{2,1,0:T(8,128)(2,1)S(1)} collective-permute-done((bf16[4,48,768]{2,1,0:T(8,128)(2,1)S(1)}, bf16[4,48,768]{2,1,0:T(8,128)(2,1)S(1)}, u32[]{:S(2)}, u32[]{:S(2)}) %collective-permute-start.15) | collective-permute-done | bytes 294944 | tf_op jit(solution)/shard_map/ppermute | solution.py:1010
  236.5 1.2 collective-permute-start.18
  237.7 3.8 %all-to-all-start.3 = ((f32[32,8,128]{2,1,0:T(8,128)}), f32[32,8,128]{2,1,0:T(8,128)S(1)}, u32[]{:S(2)}, u32[]{:S(2)}) async-start(f32[32,8,128]{2,1,0:T(8,128)} %get-tuple-element.140), calls=%async_computation.3 | async-start | bytes 262144 | tf_op jit(solution)/shard_map/all_to_all | solution.py:1238
  241.6 2.7 %collective-permute-start.20 = (bf16[48,1536]{1,0:T(8,128)(2,1)S(1)}, bf16[48,1536]{1,0:T(8,128)(2,1)S(1)}, u32[]{:S(2)}, u32[]{:S(2)}) collective-permute-start(bf16[48,1536]{1,0:T(8,128)(2,1)S(1)} %get-tuple-element.152), channel_id=1, source_target_pairs={{0,8},{1,9},{2,10},{3,11},{4,12},{5,13},{6,14},{7,15},{8,0},{9,1},... | collective-permute-start | bytes 442376 | tf_op jit(solution)/shard_map/ppermute | solution.py:1010
  244.4 1.1 collective-permute-done.18.new
  245.5 3.6 %collective-permute-start.19 = (bf16[48,1536]{1,0:T(8,128)(2,1)S(1)}, bf16[48,1536]{1,0:T(8,128)(2,1)S(1)}, u32[]{:S(2)}, u32[]{:S(2)}) collective-permute-start(bf16[48,1536]{1,0:T(8,128)(2,1)S(1)} %get-tuple-element.155), channel_id=1, source_target_pairs={{0,8},{1,9},{2,10},{3,11},{4,12},{5,13},{6,14},{7,15},{8,0},{9,1},... | collective-permute-start | bytes 442376 | tf_op jit(solution)/shard_map/ppermute | solution.py:1010
  250.4 1.2 slice.29
  251.6 4.2 %all-to-all-done.3 = f32[32,8,128]{2,1,0:T(8,128)S(1)} async-done(((f32[32,8,128]{2,1,0:T(8,128)}), f32[32,8,128]{2,1,0:T(8,128)S(1)}, u32[]{:S(2)}, u32[]{:S(2)}) %all-to-all-start.3) | async-done | bytes 131104 | tf_op jit(solution)/shard_map/all_to_all | solution.py:1238
  258.5 0.7 total.3
  259.2 1.5 collective-permute-done.19.new
  260.8 0.7 total.2
  (70 shorter events, 10.2 us)
Async XLA Ops:
  7.2 113.0 %all-gather.3.cloned.1.call-start = ((), (), s32[]{:S(2)}) async-start(), calls=%async_computation.4 | async-start | bytes 14598144 | tf_op jit(solution)/shard_map/all_gather | solution.py:1097
  11.2 105.3 %all-to-all-start = ((bf16[16,8,72]{2,1,0:T(8,128)(2,1)}), bf16[16,8,72]{2,1,0:T(8,128)(2,1)S(1)}, u32[]{:S(2)}, u32[]{:S(2)}) async-start(bf16[16,8,72]{2,1,0:T(8,128)(2,1)} %broadcast_in_dim.39), calls=%async_computation | async-start | bytes 65536 | tf_op jit(solution)/shard_map/all_to_all | solution.py:1154
  19.9 51.9 %copy-start.10 = (s32[32]{0:T(128)S(1)}, s32[32]{0:T(128)}, u32[]{:S(2)}) copy-start(s32[32]{0:T(128)} %param.30) | copy-start | bytes 388
  19.9 52.0 %copy-start.7 = (s32[1024]{0:T(1024)S(1)}, s32[1024]{0:T(1024)}, u32[]{:S(2)}) copy-start(s32[1024]{0:T(1024)} %param.31) | copy-start | bytes 12292
  69.8 7.3 %collective-permute-start = (bf16[32,768]{1,0:T(8,128)(2,1)}, bf16[32,768]{1,0:T(8,128)(2,1)S(1)}, u32[]{:S(2)}, u32[]{:S(2)}) collective-permute-start(bf16[32,768]{1,0:T(8,128)(2,1)} %image_forward.1), channel_id=1, source_target_pairs={{0,4},{1,5},{2,6},{3,7},{4,0},{5,1},{6,2},{7,3},{8,12},{9,13},{10,... | collective-permute-start | bytes 147464 | tf_op jit(solution)/shard_map/ppermute | solution.py:1010
  77.9 15.1 %collective-permute-start.1 = (bf16[64,768]{1,0:T(8,128)(2,1)S(1)}, bf16[64,768]{1,0:T(8,128)(2,1)S(1)}, u32[]{:S(2)}, u32[]{:S(2)}) collective-permute-start(bf16[64,768]{1,0:T(8,128)(2,1)S(1)} %pad_maximum_fusion.2), channel_id=1, source_target_pairs={{0,8},{1,9},{2,10},{3,11},{4,12},{5,13},{6,14},{7,15},{8,0},{9,1},... | collective-permute-start | bytes 294920 | tf_op jit(solution)/shard_map/ppermute | solution.py:1010
  93.8 8.5 %collective-permute-start.2 = (bf16[128,768]{1,0:T(8,128)(2,1)S(1)}, bf16[128,768]{1,0:T(8,128)(2,1)S(1)}, u32[]{:S(2)}, u32[]{:S(2)}) collective-permute-start(bf16[128,768]{1,0:T(8,128)(2,1)S(1)} %pad_maximum_fusion.1), channel_id=1, source_target_pairs={{0,16},{1,17},{2,18},{3,19},{4,20},{5,21},{6,22},{7,23},{8,24},{9,... | collective-permute-start | bytes 589832 | tf_op jit(solution)/shard_map/ppermute | solution.py:1010
  95.3 21.3 %copy-start.8 = (f32[1024]{0:T(1024)}, f32[1024]{0:T(1024)S(1)}, u32[]{:S(2)}) copy-start(f32[1024]{0:T(1024)S(1)} %broadcast_maximum_fusion) | copy-start | bytes 12292
  103.1 10.2 %collective-permute-start.3 = (bf16[256,768]{1,0:T(8,128)(2,1)S(1)}, bf16[256,768]{1,0:T(8,128)(2,1)S(1)}, u32[]{:S(2)}, u32[]{:S(2)}) collective-permute-start(bf16[256,768]{1,0:T(8,128)(2,1)S(1)} %pad_maximum_fusion), channel_id=1, source_target_pairs={{0,2},{1,3},{2,0},{3,1},{4,6},{5,7},{6,4},{7,5},{8,10},{9,11},{10,... | collective-permute-start | bytes 1179656 | tf_op jit(solution)/shard_map/ppermute | solution.py:1010
  114.1 3.9 %collective-permute-start.4 = (bf16[512,768]{1,0:T(8,128)(2,1)}, bf16[512,768]{1,0:T(8,128)(2,1)S(1)}, u32[]{:S(2)}, u32[]{:S(2)}) collective-permute-start(bf16[512,768]{1,0:T(8,128)(2,1)} %get-tuple-element.158), channel_id=1, source_target_pairs={{0,1},{1,0},{2,3},{3,2},{4,5},{5,4},{6,7},{7,6},{8,9},{9,8},{10,11... | collective-permute-start | bytes 2359304 | tf_op jit(solution)/shard_map/ppermute | solution.py:1010
  142.5 13.5 %all-to-all-start.1 = ((f32[32,8,128]{2,1,0:T(8,128)}), f32[32,8,128]{2,1,0:T(8,128)S(1)}, u32[]{:S(2)}, u32[]{:S(2)}) async-start(f32[32,8,128]{2,1,0:T(8,128)} %get-tuple-element.84), calls=%async_computation.1 | async-start | bytes 262144 | tf_op jit(solution)/shard_map/all_to_all | solution.py:1194
  156.0 0.7 copy-start.6
  172.4 3.5 %collective-permute-start.5 = (bf16[2,2,4,48,768]{4,3,2,1,0:T(8,128)(2,1)}, bf16[2,2,4,48,768]{4,3,2,1,0:T(8,128)(2,1)}, u32[]{:S(2)}, u32[]{:S(2)}) collective-permute-start(bf16[2,2,4,48,768]{4,3,2,1,0:T(8,128)(2,1)} %get-tuple-element.101), channel_id=1, source_target_pairs={{0,1},{1,0},{2,3},{3,2},{4,5},{5,4},{6,7},{7,6},{8,9},{9,8},{10,11... | collective-permute-start | bytes 3538952 | tf_op jit(solution)/shard_map/ppermute | solution.py:1010
  172.7 4.6 %collective-permute-start.6 = (bf16[2,2,4,48,768]{4,3,2,1,0:T(8,128)(2,1)}, bf16[2,2,4,48,768]{4,3,2,1,0:T(8,128)(2,1)}, u32[]{:S(2)}, u32[]{:S(2)}) collective-permute-start(bf16[2,2,4,48,768]{4,3,2,1,0:T(8,128)(2,1)} %get-tuple-element.103), channel_id=1, source_target_pairs={{0,1},{1,0},{2,3},{3,2},{4,5},{5,4},{6,7},{7,6},{8,9},{9,8},{10,11... | collective-permute-start | bytes 3538952 | tf_op jit(solution)/shard_map/ppermute | solution.py:1010
  173.0 35.5 %all-to-all-start.2 = ((bf16[32,32,576]{2,1,0:T(8,128)(2,1)}), bf16[32,32,576]{2,1,0:T(8,128)(2,1)S(1)}, u32[]{:S(2)}, u32[]{:S(2)}) async-start(bf16[32,32,576]{2,1,0:T(8,128)(2,1)} %get-tuple-element.122), calls=%async_computation.2 | async-start | bytes 2621440 | tf_op jit(solution)/shard_map/all_to_all | solution.py:1210
  190.0 3.1 %collective-permute-start.7 = (bf16[2,2,4,48,768]{4,3,2,1,0:T(8,128)(2,1)}, bf16[2,2,4,48,768]{4,3,2,1,0:T(8,128)(2,1)S(1)}, u32[]{:S(2)}, u32[]{:S(2)}) collective-permute-start(bf16[2,2,4,48,768]{4,3,2,1,0:T(8,128)(2,1)} %get-tuple-element.108), channel_id=1, source_target_pairs={{0,1},{1,0},{2,3},{3,2},{4,5},{5,4},{6,7},{7,6},{8,9},{9,8},{10,11... | collective-permute-start | bytes 3538952 | tf_op jit(solution)/shard_map/ppermute | solution.py:1010
  190.3 4.5 %collective-permute-start.8 = (bf16[2,2,4,48,768]{4,3,2,1,0:T(8,128)(2,1)}, bf16[2,2,4,48,768]{4,3,2,1,0:T(8,128)(2,1)S(1)}, u32[]{:S(2)}, u32[]{:S(2)}) collective-permute-start(bf16[2,2,4,48,768]{4,3,2,1,0:T(8,128)(2,1)} %get-tuple-element.110), channel_id=1, source_target_pairs={{0,1},{1,0},{2,3},{3,2},{4,5},{5,4},{6,7},{7,6},{8,9},{9,8},{10,11... | collective-permute-start | bytes 3538952 | tf_op jit(solution)/shard_map/ppermute | solution.py:1010
  190.6 28.3 %collective-permute-start.9 = (bf16[2,4,48,768]{3,2,1,0:T(8,128)(2,1)}, bf16[2,4,48,768]{3,2,1,0:T(8,128)(2,1)}, u32[]{:S(2)}, u32[]{:S(2)}) collective-permute-start(bf16[2,4,48,768]{3,2,1,0:T(8,128)(2,1)} %get-tuple-element.127), channel_id=1, source_target_pairs={{0,16},{1,17},{2,18},{3,19},{4,20},{5,21},{6,22},{7,23},{8,24},{9,... | collective-permute-start | bytes 1769480 | tf_op jit(solution)/shard_map/ppermute | solution.py:1010
  191.4 27.5 %collective-permute-start.10 = (bf16[2,4,48,768]{3,2,1,0:T(8,128)(2,1)}, bf16[2,4,48,768]{3,2,1,0:T(8,128)(2,1)}, u32[]{:S(2)}, u32[]{:S(2)}) collective-permute-start(bf16[2,4,48,768]{3,2,1,0:T(8,128)(2,1)} %get-tuple-element.129), channel_id=1, source_target_pairs={{0,2},{1,3},{2,0},{3,1},{4,6},{5,7},{6,4},{7,5},{8,10},{9,11},{10,... | collective-permute-start | bytes 1769480 | tf_op jit(solution)/shard_map/ppermute | solution.py:1010
  194.8 1.3 copy-start
  196.1 1.3 copy-start.1
  199.0 0.8 copy-start.4
  199.8 22.8 %collective-permute-start.11 = (bf16[2,4,48,768]{3,2,1,0:T(8,128)(2,1)}, bf16[2,4,48,768]{3,2,1,0:T(8,128)(2,1)}, u32[]{:S(2)}, u32[]{:S(2)}) collective-permute-start(bf16[2,4,48,768]{3,2,1,0:T(8,128)(2,1)} %bitcast.21), channel_id=1, source_target_pairs={{0,16},{1,17},{2,18},{3,19},{4,20},{5,21},{6,22},{7,23},{8,24},{9,... | collective-permute-start | bytes 1769480 | tf_op jit(solution)/shard_map/ppermute | solution.py:1010
  200.6 23.5 %collective-permute-start.12 = (bf16[2,4,48,768]{3,2,1,0:T(8,128)(2,1)}, bf16[2,4,48,768]{3,2,1,0:T(8,128)(2,1)}, u32[]{:S(2)}, u32[]{:S(2)}) collective-permute-start(bf16[2,4,48,768]{3,2,1,0:T(8,128)(2,1)} %bitcast.23), channel_id=1, source_target_pairs={{0,2},{1,3},{2,0},{3,1},{4,6},{5,7},{6,4},{7,5},{8,10},{9,11},{10,... | collective-permute-start | bytes 1769480 | tf_op jit(solution)/shard_map/ppermute | solution.py:1010
  209.6 9.3 %copy-start.2 = (bf16[2,4,48,768]{3,2,1,0:T(8,128)(2,1)S(1)}, bf16[2,4,48,768]{3,2,1,0:T(8,128)(2,1)}, u32[]{:S(2)}) copy-start(bf16[2,4,48,768]{3,2,1,0:T(8,128)(2,1)} %get-tuple-element.126.a_own) | copy-start | bytes 1769476
  209.6 9.3 %copy-start.3 = (bf16[2,4,48,768]{3,2,1,0:T(8,128)(2,1)S(1)}, bf16[2,4,48,768]{3,2,1,0:T(8,128)(2,1)}, u32[]{:S(2)}) copy-start(bf16[2,4,48,768]{3,2,1,0:T(8,128)(2,1)} %get-tuple-element.128.b_own) | copy-start | bytes 1769476
  218.9 5.2 %copy-start.5 = (bf16[8,48,768]{2,1,0:T(8,128)(2,1)S(1)}, bf16[8,48,768]{2,1,0:T(8,128)(2,1)}, u32[]{:S(2)}) copy-start(bf16[8,48,768]{2,1,0:T(8,128)(2,1)} %copy-done.4) | copy-start | bytes 1769476
  220.5 10.0 %collective-permute-start.13 = (bf16[4,48,768]{2,1,0:T(8,128)(2,1)S(1)}, bf16[4,48,768]{2,1,0:T(8,128)(2,1)S(1)}, u32[]{:S(2)}, u32[]{:S(2)}) collective-permute-start(bf16[4,48,768]{2,1,0:T(8,128)(2,1)S(1)} %get-tuple-element.131), channel_id=1, source_target_pairs={{0,2},{1,3},{2,0},{3,1},{4,6},{5,7},{6,4},{7,5},{8,10},{9,11},{10,... | collective-permute-start | bytes 884744 | tf_op jit(solution)/shard_map/ppermute | solution.py:1010
  222.1 8.6 %collective-permute-start.14 = (bf16[4,48,768]{2,1,0:T(8,128)(2,1)S(1)}, bf16[4,48,768]{2,1,0:T(8,128)(2,1)S(1)}, u32[]{:S(2)}, u32[]{:S(2)}) collective-permute-start(bf16[4,48,768]{2,1,0:T(8,128)(2,1)S(1)} %get-tuple-element.133), channel_id=1, source_target_pairs={{0,16},{1,17},{2,18},{3,19},{4,20},{5,21},{6,22},{7,23},{8,24},{9,... | collective-permute-start | bytes 884744 | tf_op jit(solution)/shard_map/ppermute | solution.py:1010
  225.6 10.7 %collective-permute-start.15 = (bf16[4,48,768]{2,1,0:T(8,128)(2,1)S(1)}, bf16[4,48,768]{2,1,0:T(8,128)(2,1)S(1)}, u32[]{:S(2)}, u32[]{:S(2)}) collective-permute-start(bf16[4,48,768]{2,1,0:T(8,128)(2,1)S(1)} %get-tuple-element.137), channel_id=1, source_target_pairs={{0,2},{1,3},{2,0},{3,1},{4,6},{5,7},{6,4},{7,5},{8,10},{9,11},{10,... | collective-permute-start | bytes 884744 | tf_op jit(solution)/shard_map/ppermute | solution.py:1010
  225.8 10.6 %collective-permute-start.16 = (bf16[4,48,768]{2,1,0:T(8,128)(2,1)S(1)}, bf16[4,48,768]{2,1,0:T(8,128)(2,1)S(1)}, u32[]{:S(2)}, u32[]{:S(2)}) collective-permute-start(bf16[4,48,768]{2,1,0:T(8,128)(2,1)S(1)} %get-tuple-element.139), channel_id=1, source_target_pairs={{0,16},{1,17},{2,18},{3,19},{4,20},{5,21},{6,22},{7,23},{8,24},{9,... | collective-permute-start | bytes 884744 | tf_op jit(solution)/shard_map/ppermute | solution.py:1010
  230.9 10.7 %collective-permute-start.17 = (bf16[2,48,1536]{2,1,0:T(8,128)(2,1)S(1)}, bf16[2,48,1536]{2,1,0:T(8,128)(2,1)S(1)}, u32[]{:S(2)}, u32[]{:S(2)}) collective-permute-start(bf16[2,48,1536]{2,1,0:T(8,128)(2,1)S(1)} %get-tuple-element.145), channel_id=1, source_target_pairs={{0,4},{1,5},{2,6},{3,7},{4,0},{5,1},{6,2},{7,3},{8,12},{9,13},{10,... | collective-permute-start | bytes 884744 | tf_op jit(solution)/shard_map/ppermute | solution.py:1010
  236.5 9.0 %collective-permute-start.18 = (bf16[2,48,1536]{2,1,0:T(8,128)(2,1)S(1)}, bf16[2,48,1536]{2,1,0:T(8,128)(2,1)S(1)}, u32[]{:S(2)}, u32[]{:S(2)}) collective-permute-start(bf16[2,48,1536]{2,1,0:T(8,128)(2,1)S(1)} %get-tuple-element.149), channel_id=1, source_target_pairs={{0,4},{1,5},{2,6},{3,7},{4,0},{5,1},{6,2},{7,3},{8,12},{9,13},{10,... | collective-permute-start | bytes 884744 | tf_op jit(solution)/shard_map/ppermute | solution.py:1010
  237.7 18.1 %all-to-all-start.3 = ((f32[32,8,128]{2,1,0:T(8,128)}), f32[32,8,128]{2,1,0:T(8,128)S(1)}, u32[]{:S(2)}, u32[]{:S(2)}) async-start(f32[32,8,128]{2,1,0:T(8,128)} %get-tuple-element.140), calls=%async_computation.3 | async-start | bytes 262144 | tf_op jit(solution)/shard_map/all_to_all | solution.py:1238
  241.6 16.9 %collective-permute-start.20 = (bf16[48,1536]{1,0:T(8,128)(2,1)S(1)}, bf16[48,1536]{1,0:T(8,128)(2,1)S(1)}, u32[]{:S(2)}, u32[]{:S(2)}) collective-permute-start(bf16[48,1536]{1,0:T(8,128)(2,1)S(1)} %get-tuple-element.152), channel_id=1, source_target_pairs={{0,8},{1,9},{2,10},{3,11},{4,12},{5,13},{6,14},{7,15},{8,0},{9,1},... | collective-permute-start | bytes 442376 | tf_op jit(solution)/shard_map/ppermute | solution.py:1010
  245.5 15.3 %collective-permute-start.19 = (bf16[48,1536]{1,0:T(8,128)(2,1)S(1)}, bf16[48,1536]{1,0:T(8,128)(2,1)S(1)}, u32[]{:S(2)}, u32[]{:S(2)}) collective-permute-start(bf16[48,1536]{1,0:T(8,128)(2,1)S(1)} %get-tuple-element.155), channel_id=1, source_target_pairs={{0,8},{1,9},{2,10},{3,11},{4,12},{5,13},{6,14},{7,15},{8,0},{9,1},... | collective-permute-start | bytes 442376 | tf_op jit(solution)/shard_map/ppermute | solution.py:1010
  255.8 5.6 %copy-start.9 = (f32[8,128]{1,0:T(8,128)}, f32[8,128]{1,0:T(8,128)S(1)}, u32[]{:S(2)}) copy-start(f32[8,128]{1,0:T(8,128)S(1)} %reduce_sum.28) | copy-start | bytes 12292
Sparse Core Ops, SparseCore 0:
  10.9 108.2 all-gather.2
where the time goes:
time: 270 us; the launch traced here: 269 us
  Pallas kernels  122 us (45%)
  waiting for transfers between devices  61.1 us (23%)
  starting transfers between devices  43.3 us (16%)
  local copies, waits for them, and re-layouts  18.1 us (7%)
  between operations  17.4 us (6%)
  other arithmetic  6.66 us (2%)
    pallas_call x1, Pallas kernels, image_forward(): pl.pallas_call(image_kernel, name='image_forward', grid=(pairs // group,)...  49.9 us
    ppermute x21, waiting for transfers between devices, hop(): return lax.ppermute(array, AXES, shifted(x, y, z, core))  45.7 us
    ppermute x21, starting transfers between devices, hop(): return lax.ppermute(array, AXES, shifted(x, y, z, core))  23.9 us
    pallas_call x1, Pallas kernels, text_forward(): pl.pallas_call(functools.partial(text_forward_kernel, length), name='text...  22.3 us
    pallas_call x1, Pallas kernels, back_one(): pl.pallas_call(functools.partial(back_one_kernel, length, shard), name='b...  15.8 us
    pallas_call x1, Pallas kernels, back_two(): pl.pallas_call(functools.partial(back_two_kernel, length), name='back_two...  12.7 us
    pallas_call x1, Pallas kernels, back_third(): pl.pallas_call(functools.partial(back_third_kernel, shard[1]), name='back...  9.27 us
    unnamed x26, local copies, waits for them, and re-layouts  7.46 us
  transfers between devices with their start and end apart: 26, of which 16 were waited for; matrix products, arithmetic and copies ran while one was open for 8% of the time, Pallas kernels for 30%

commit v1 on v0

--- a/solution.py
+++ b/solution.py
@@ -766,7 +766,7 @@
                 low_lane, dv[:blk], dv[blk:]
             ).astype(BF)
 
-    repeat(rows // blk, group, 2)
+    repeat(rows // blk, group)
     sums[0:1, :] = jnp.sum(dqkv[:, :width].astype(F32), axis=0, keepdims=True)
     sums[1:2, :] = jnp.sum(dqkv[:, 2 * width :].astype(F32), axis=0, keepdims=True)
     sums[2:8, :] = jnp.zeros((6, width), F32)
@@ -804,7 +804,7 @@
             part = dqkv[:, pl.ds(pl.multiple_of(first + c, 128), 256)]
             put_grad(dot(h1_t[...], part), parts, x, c, 0)
 
-        repeat(width // 256, chunk, 3)
+        repeat(width // 256, chunk)
         part = dqkv[:, pl.ds(pl.multiple_of(first + width, 128), piece)]
         put_grad(dot(h1_t[...], part), parts, x, 0, 1)
         part = dz[:, pl.ds(pl.multiple_of(other * piece, 128), piece)]

time: 270 us -> 271 us (level)
    all_to_all x1, waiting for transfers between devices: 4.2 us -> 0.01 us  [body(): share = jnp.sum(lax.all_to_all(share, AXES, 0, 0, tiled=True), axis=0)]
    ppermute x21, waiting for transfers between devices: 45.7 us -> 49.2 us  [hop(): return lax.ppermute(array, AXES, shifted(x, y, z, core))]
  transfers between devices with their start and end apart: 26 -> 26, of which waited for: 16 -> 17; matrix products, arithmetic and copies ran while one was open for 8% -> 8% of each run, Pallas kernels for 30% -> 31%
where the time goes in v1:
time: 271 us; the launch traced here: 270 us
  Pallas kernels  123 us (45%)
  waiting for transfers between devices  59 us (22%)
  starting transfers between devices  44.7 us (16%)
  local copies, waits for them, and re-layouts  18.1 us (7%)
  between operations  17.4 us (6%)
  other arithmetic  6.66 us (2%)
    pallas_call x1, Pallas kernels, image_forward(): pl.pallas_call(image_kernel, name='image_forward', grid=(pairs // group,)...  49.9 us
    ppermute x21, waiting for transfers between devices, hop(): return lax.ppermute(array, AXES, shifted(x, y, z, core))  49.2 us
    ppermute x21, starting transfers between devices, hop(): return lax.ppermute(array, AXES, shifted(x, y, z, core))  25.6 us
    pallas_call x1, Pallas kernels, text_forward(): pl.pallas_call(functools.partial(text_forward_kernel, length), name='text...  22.3 us
    pallas_call x1, Pallas kernels, back_one(): pl.pallas_call(functools.partial(back_one_kernel, length, shard), name='b...  15.8 us
    pallas_call x1, Pallas kernels, back_two(): pl.pallas_call(functools.partial(back_two_kernel, length), name='back_two...  14.1 us
    pallas_call x1, Pallas kernels, back_third(): pl.pallas_call(functools.partial(back_third_kernel, shard[1]), name='back...  9.27 us
    unnamed x26, local copies, waits for them, and re-layouts  7.46 us
  transfers between devices with their start and end apart: 26, of which 17 were waited for; matrix products, arithmetic and copies ran while one was open for 8% of the time, Pallas kernels for 31%

profile of v1, /device:TPU:0, one launch (start us, length us, event | category | flops | bytes accessed | tf_op | source)
XLA Modules:
  0.0 270.2 jit_solution(15674969856001546801)
XLA Ops:
  7.2 1.9 pack_block.1
  9.1 0.7 reshape.197
  9.8 0.8 pad_maximum_fusion.3
  11.2 7.4 %all-to-all-start = ((bf16[16,8,72]{2,1,0:T(8,128)(2,1)}), bf16[16,8,72]{2,1,0:T(8,128)(2,1)S(1)}, u32[]{:S(2)}, u32[]{:S(2)}) async-start(bf16[16,8,72]{2,1,0:T(8,128)(2,1)} %broadcast_in_dim.39), calls=%async_computation | async-start | bytes 65536 | tf_op jit(solution)/shard_map/all_to_all | solution.py:1154
  18.6 1.3 reshape.200.ub
  19.9 49.9 %image_forward.1 = bf16[32,768]{1,0:T(8,128)(2,1)} custom-call(bf16[50,32,768]{2,1,0:T(8,128)(2,1)} %bitcast.52, bf16[768,2304]{1,0:T(8,128)(2,1)} %wq_h.1, bf16[768,768]{1,0:T(8,128)(2,1)} %wo_h.1, bf16[768,3072]{1,0:T(8,128)(2,1)} %wu_h.1, bf16[3072,768]{1,0:T(8,128)(2,1)} %wd_h.1, bf16[8,768]{1,0:T(8,128)(2,1)} %vec.1, bf16[1,3072]{1,0:T(2,128)(2,1)} %reshape.200.ub), custom_call_target="tpu_custom_call" | custom-call | flops 15099494400 | bytes 16613376 | tf_op jit(solution)/shard_map/image_forward/pallas_call | solution.py:229
  69.8 2.0 collective-permute-start
  72.5 4.6 %collective-permute-done = bf16[32,768]{1,0:T(8,128)(2,1)S(1)} collective-permute-done((bf16[32,768]{1,0:T(8,128)(2,1)}, bf16[32,768]{1,0:T(8,128)(2,1)S(1)}, u32[]{:S(2)}, u32[]{:S(2)}) %collective-permute-start) | collective-permute-done | bytes 49184 | tf_op jit(solution)/shard_map/ppermute | solution.py:1010
  77.1 0.8 pad_maximum_fusion.2
  77.9 2.1 collective-permute-start.1
  80.0 1.4 constant_dynamic-update-slice_fusion.4
  81.4 11.6 %collective-permute-done.1 = bf16[64,768]{1,0:T(8,128)(2,1)S(1)} collective-permute-done((bf16[64,768]{1,0:T(8,128)(2,1)S(1)}, bf16[64,768]{1,0:T(8,128)(2,1)S(1)}, u32[]{:S(2)}, u32[]{:S(2)}) %collective-permute-start.1) | collective-permute-done | bytes 98336 | tf_op jit(solution)/shard_map/ppermute | solution.py:1010
  93.0 0.8 pad_maximum_fusion.1
  93.8 1.5 collective-permute-start.2
  95.3 7.0 %collective-permute-done.2 = bf16[128,768]{1,0:T(8,128)(2,1)S(1)} collective-permute-done((bf16[128,768]{1,0:T(8,128)(2,1)S(1)}, bf16[128,768]{1,0:T(8,128)(2,1)S(1)}, u32[]{:S(2)}, u32[]{:S(2)}) %collective-permute-start.2) | collective-permute-done | bytes 196640 | tf_op jit(solution)/shard_map/ppermute | solution.py:1010
  102.3 0.8 pad_maximum_fusion
  103.1 1.5 collective-permute-start.3
  105.9 0.7 constant_dynamic-update-slice_fusion.1
  106.6 6.7 %collective-permute-done.3 = bf16[256,768]{1,0:T(8,128)(2,1)S(1)} collective-permute-done((bf16[256,768]{1,0:T(8,128)(2,1)S(1)}, bf16[256,768]{1,0:T(8,128)(2,1)S(1)}, u32[]{:S(2)}, u32[]{:S(2)}) %collective-permute-start.3) | collective-permute-done | bytes 393248 | tf_op jit(solution)/shard_map/ppermute | solution.py:1010
  113.3 0.8 constant_dynamic-update-slice_fusion
  115.1 0.7 copy.36.own_group
  116.6 0.7 reshape.199.ub
  117.3 0.7 reshape.198.vec
  118.8 1.4 bitcast_select_fusion.images_i
  120.2 22.3 %text_forward.1 = (bf16[512,768]{1,0:T(8,128)(2,1)}, bf16[512,2304]{1,0:T(8,128)(2,1)}, bf16[512,768]{1,0:T(8,128)(2,1)}, f32[512,768]{1,0:T(8,128)}, bf16[512,7...) custom-call(bf16[512,768]{1,0:T(8,128)(2,1)} %bitcast.45, ...), custom_call_target="tpu_custom_call" | custom-call | flops 4831838208 | bytes 23592960 | tf_op jit(solution)/shard_map/text_forward/pallas_call | solution.py:446
  142.5 5.2 %all-to-all-start.1 = ((f32[32,8,128]{2,1,0:T(8,128)}), f32[32,8,128]{2,1,0:T(8,128)S(1)}, u32[]{:S(2)}, u32[]{:S(2)}) async-start(f32[32,8,128]{2,1,0:T(8,128)} %get-tuple-element.84), calls=%async_computation.1 | async-start | bytes 262144 | tf_op jit(solution)/shard_map/all_to_all | solution.py:1194
  148.4 3.5 %relative_rows.1 = (bf16[768,512]{1,0:T(8,128)(2,1)}, bf16[768,512]{1,0:T(8,128)(2,1)}, bf16[768,512]{1,0:T(8,128)(2,1)}) custom-call(s32[4]{0:T(128)} %pad_add_fusion.where, bf16[512,768]{1,0:T(8,128)(2,1)} %get-tuple-element.88.h1_i, bf16[512,768]{1,0:T(8,128)(2,1)} %get-tuple-element.89.h2_i, bf16[512,768]{1,0:T(8,128)(2,1)} %get-tuple-element.90.att_i), custom_call_target="tpu_custom_call" | custom-call | bytes 4718592 | tf_op jit(solution)/shard_map/relative_rows/pallas_call | solution.py:515
  152.0 4.0 %all-to-all-done.1.row_all = f32[32,8,128]{2,1,0:T(8,128)S(1)} async-done(((f32[32,8,128]{2,1,0:T(8,128)}), f32[32,8,128]{2,1,0:T(8,128)S(1)}, u32[]{:S(2)}, u32[]{:S(2)}) %all-to-all-start.1) | async-done | bytes 131104 | tf_op jit(solution)/shard_map/all_to_all | solution.py:1194
  156.6 15.8 %back_one.1 = (bf16[32,32,576]{2,1,0:T(8,128)(2,1)}, bf16[2,2,4,48,768]{4,3,2,1,0:T(8,128)(2,1)}, bf16[2,2,4,48,768]{4,3,2,1,0:T(8,128)(2,1)}, bf16[2,2,4,48,768...) custom-call(s32[4]{0:T(128)} %pad_add_fusion.where, ...), custom_call_target="tpu_custom_call" | custom-call | flops 5435817984 | bytes 37748736 | tf_op jit(solution)/shard_map/back_one/pallas_call | solution.py:674
  173.0 2.9 %all-to-all-start.2 = ((bf16[32,32,576]{2,1,0:T(8,128)(2,1)}), bf16[32,32,576]{2,1,0:T(8,128)(2,1)S(1)}, u32[]{:S(2)}, u32[]{:S(2)}) async-start(bf16[32,32,576]{2,1,0:T(8,128)(2,1)} %get-tuple-element.122), calls=%async_computation.2 | async-start | bytes 2621440 | tf_op jit(solution)/shard_map/all_to_all | solution.py:1210
  175.9 1.5 collective-permute-done.6.up_b_new
  177.3 14.1 %back_two.1 = (bf16[512,2304]{1,0:T(8,128)(2,1)}, bf16[2,2,4,48,768]{4,3,2,1,0:T(8,128)(2,1)}, bf16[2,2,4,48,768]{4,3,2,1,0:T(8,128)(2,1)}, bf16[2,2,4,48,768]{4...) custom-call(s32[4]{0:T(128)} %pad_add_fusion.where, ...), custom_call_target="tpu_custom_call" | custom-call | flops 3422552064 | bytes 7864320 | tf_op jit(solution)/shard_map/back_two/pallas_call | solution.py:821
  192.0 0.8 collective-permute-start.9
  192.8 0.7 collective-permute-start.10
  193.5 1.1 collective-permute-done.7
  194.6 1.7 collective-permute-done.8
  196.2 1.3 copy-done
  197.5 1.3 copy-done.1
  198.8 1.6 fold.3
  200.4 0.8 copy-done.4
  201.3 0.8 collective-permute-start.11
  202.0 0.7 collective-permute-start.12
  202.7 5.8 %all-to-all-done.2 = bf16[32,32,576]{2,1,0:T(8,128)(2,1)S(1)} async-done(((bf16[32,32,576]{2,1,0:T(8,128)(2,1)}), bf16[32,32,576]{2,1,0:T(8,128)(2,1)S(1)}, u32[]{:S(2)}, u32[]{:S(2)}) %all-to-all-start.2) | async-done | bytes 1179680 | tf_op jit(solution)/shard_map/all_to_all | solution.py:1210
  208.5 1.1 fusion
  209.6 9.3 %back_third.1 = (f32[512,768]{1,0:T(8,128)}, f32[32,8,128]{2,1,0:T(8,128)}) custom-call(f32[512,768]{1,0:T(8,128)} %get-tuple-element.94.dr1_i, bf16[512,2304]{1,0:T(8,128)(2,1)} %get-tuple-element.115.dqkv_i, bf16[512,768]{1,0:T(8,128)(2,1)} %bitcast.46, bf16[32,576,384]{2,1,0:T(8,128)(2,1)} %bitcast.42, bf16[8,768]{1,0:T(8,128)(2,1)} %reshape.198.vec, ...), custom_call_target="tpu_custom_call" | custom-call | flops 1811939328 | bytes 8257536 | tf_op jit(solution)/shard_map/back_third/pallas_call | solution.py:903
  219.0 1.6 fold.4
  220.5 1.6 collective-permute-start.13
  222.6 2.0 collective-permute-done.11.a_new
  225.0 1.5 fold.5
  226.6 1.0 collective-permute-start.15
  227.6 1.1 collective-permute-start.16
  228.6 2.6 collective-permute-done.13.a_new
  231.9 1.3 collective-permute-start.17
  233.1 3.5 %collective-permute-done.15.a_new = bf16[4,48,768]{2,1,0:T(8,128)(2,1)S(1)} collective-permute-done((bf16[4,48,768]{2,1,0:T(8,128)(2,1)S(1)}, bf16[4,48,768]{2,1,0:T(8,128)(2,1)S(1)}, u32[]{:S(2)}, u32[]{:S(2)}) %collective-permute-start.15) | collective-permute-done | bytes 294944 | tf_op jit(solution)/shard_map/ppermute | solution.py:1010
  236.7 2.0 collective-permute-start.18
  238.7 3.5 %all-to-all-start.3 = ((f32[32,8,128]{2,1,0:T(8,128)}), f32[32,8,128]{2,1,0:T(8,128)S(1)}, u32[]{:S(2)}, u32[]{:S(2)}) async-start(f32[32,8,128]{2,1,0:T(8,128)} %get-tuple-element.140), calls=%async_computation.3 | async-start | bytes 262144 | tf_op jit(solution)/shard_map/all_to_all | solution.py:1238
  242.3 2.7 %collective-permute-start.20 = (bf16[48,1536]{1,0:T(8,128)(2,1)S(1)}, bf16[48,1536]{1,0:T(8,128)(2,1)S(1)}, u32[]{:S(2)}, u32[]{:S(2)}) collective-permute-start(bf16[48,1536]{1,0:T(8,128)(2,1)S(1)} %get-tuple-element.152), channel_id=1, source_target_pairs={{0,8},{1,9},{2,10},{3,11},{4,12},{5,13},{6,14},{7,15},{8,0},{9,1},... | collective-permute-start | bytes 442376 | tf_op jit(solution)/shard_map/ppermute | solution.py:1010
  245.1 0.8 collective-permute-done.18.new
  245.9 4.2 %collective-permute-start.19 = (bf16[48,1536]{1,0:T(8,128)(2,1)S(1)}, bf16[48,1536]{1,0:T(8,128)(2,1)S(1)}, u32[]{:S(2)}, u32[]{:S(2)}) collective-permute-start(bf16[48,1536]{1,0:T(8,128)(2,1)S(1)} %get-tuple-element.155), channel_id=1, source_target_pairs={{0,8},{1,9},{2,10},{3,11},{4,12},{5,13},{6,14},{7,15},{8,0},{9,1},... | collective-permute-start | bytes 442376 | tf_op jit(solution)/shard_map/ppermute | solution.py:1010
  251.4 1.2 slice.29
  255.3 3.5 %collective-permute-done.20.new = bf16[48,1536]{1,0:T(8,128)(2,1)S(1)} collective-permute-done((bf16[48,1536]{1,0:T(8,128)(2,1)S(1)}, bf16[48,1536]{1,0:T(8,128)(2,1)S(1)}, u32[]{:S(2)}, u32[]{:S(2)}) %collective-permute-start.20) | collective-permute-done | bytes 147488 | tf_op jit(solution)/shard_map/ppermute | solution.py:1010
  258.8 0.7 total.3
  259.5 1.9 collective-permute-done.19.new
  261.5 0.7 total.2
  (70 shorter events, 11.4 us)
Async XLA Ops:
  7.2 113.0 %all-gather.3.cloned.1.call-start = ((), (), s32[]{:S(2)}) async-start(), calls=%async_computation.4 | async-start | bytes 14598144 | tf_op jit(solution)/shard_map/all_gather | solution.py:1097
  11.2 105.3 %all-to-all-start = ((bf16[16,8,72]{2,1,0:T(8,128)(2,1)}), bf16[16,8,72]{2,1,0:T(8,128)(2,1)S(1)}, u32[]{:S(2)}, u32[]{:S(2)}) async-start(bf16[16,8,72]{2,1,0:T(8,128)(2,1)} %broadcast_in_dim.39), calls=%async_computation | async-start | bytes 65536 | tf_op jit(solution)/shard_map/all_to_all | solution.py:1154
  19.9 51.9 %copy-start.10 = (s32[32]{0:T(128)S(1)}, s32[32]{0:T(128)}, u32[]{:S(2)}) copy-start(s32[32]{0:T(128)} %param.30) | copy-start | bytes 388
  19.9 52.0 %copy-start.7 = (s32[1024]{0:T(1024)S(1)}, s32[1024]{0:T(1024)}, u32[]{:S(2)}) copy-start(s32[1024]{0:T(1024)} %param.31) | copy-start | bytes 12292
  69.8 7.3 %collective-permute-start = (bf16[32,768]{1,0:T(8,128)(2,1)}, bf16[32,768]{1,0:T(8,128)(2,1)S(1)}, u32[]{:S(2)}, u32[]{:S(2)}) collective-permute-start(bf16[32,768]{1,0:T(8,128)(2,1)} %image_forward.1), channel_id=1, source_target_pairs={{0,4},{1,5},{2,6},{3,7},{4,0},{5,1},{6,2},{7,3},{8,12},{9,13},{10,... | collective-permute-start | bytes 147464 | tf_op jit(solution)/shard_map/ppermute | solution.py:1010
  77.9 15.1 %collective-permute-start.1 = (bf16[64,768]{1,0:T(8,128)(2,1)S(1)}, bf16[64,768]{1,0:T(8,128)(2,1)S(1)}, u32[]{:S(2)}, u32[]{:S(2)}) collective-permute-start(bf16[64,768]{1,0:T(8,128)(2,1)S(1)} %pad_maximum_fusion.2), channel_id=1, source_target_pairs={{0,8},{1,9},{2,10},{3,11},{4,12},{5,13},{6,14},{7,15},{8,0},{9,1},... | collective-permute-start | bytes 294920 | tf_op jit(solution)/shard_map/ppermute | solution.py:1010
  93.8 8.5 %collective-permute-start.2 = (bf16[128,768]{1,0:T(8,128)(2,1)S(1)}, bf16[128,768]{1,0:T(8,128)(2,1)S(1)}, u32[]{:S(2)}, u32[]{:S(2)}) collective-permute-start(bf16[128,768]{1,0:T(8,128)(2,1)S(1)} %pad_maximum_fusion.1), channel_id=1, source_target_pairs={{0,16},{1,17},{2,18},{3,19},{4,20},{5,21},{6,22},{7,23},{8,24},{9,... | collective-permute-start | bytes 589832 | tf_op jit(solution)/shard_map/ppermute | solution.py:1010
  95.3 21.3 %copy-start.8 = (f32[1024]{0:T(1024)}, f32[1024]{0:T(1024)S(1)}, u32[]{:S(2)}) copy-start(f32[1024]{0:T(1024)S(1)} %broadcast_maximum_fusion) | copy-start | bytes 12292
  103.1 10.2 %collective-permute-start.3 = (bf16[256,768]{1,0:T(8,128)(2,1)S(1)}, bf16[256,768]{1,0:T(8,128)(2,1)S(1)}, u32[]{:S(2)}, u32[]{:S(2)}) collective-permute-start(bf16[256,768]{1,0:T(8,128)(2,1)S(1)} %pad_maximum_fusion), channel_id=1, source_target_pairs={{0,2},{1,3},{2,0},{3,1},{4,6},{5,7},{6,4},{7,5},{8,10},{9,11},{10,... | collective-permute-start | bytes 1179656 | tf_op jit(solution)/shard_map/ppermute | solution.py:1010
  114.1 3.9 %collective-permute-start.4 = (bf16[512,768]{1,0:T(8,128)(2,1)}, bf16[512,768]{1,0:T(8,128)(2,1)S(1)}, u32[]{:S(2)}, u32[]{:S(2)}) collective-permute-start(bf16[512,768]{1,0:T(8,128)(2,1)} %get-tuple-element.158), channel_id=1, source_target_pairs={{0,1},{1,0},{2,3},{3,2},{4,5},{5,4},{6,7},{7,6},{8,9},{9,8},{10,11... | collective-permute-start | bytes 2359304 | tf_op jit(solution)/shard_map/ppermute | solution.py:1010
  142.5 13.5 %all-to-all-start.1 = ((f32[32,8,128]{2,1,0:T(8,128)}), f32[32,8,128]{2,1,0:T(8,128)S(1)}, u32[]{:S(2)}, u32[]{:S(2)}) async-start(f32[32,8,128]{2,1,0:T(8,128)} %get-tuple-element.84), calls=%async_computation.1 | async-start | bytes 262144 | tf_op jit(solution)/shard_map/all_to_all | solution.py:1194
  156.0 0.7 copy-start.6
  172.4 3.5 %collective-permute-start.5 = (bf16[2,2,4,48,768]{4,3,2,1,0:T(8,128)(2,1)}, bf16[2,2,4,48,768]{4,3,2,1,0:T(8,128)(2,1)}, u32[]{:S(2)}, u32[]{:S(2)}) collective-permute-start(bf16[2,2,4,48,768]{4,3,2,1,0:T(8,128)(2,1)} %get-tuple-element.101), channel_id=1, source_target_pairs={{0,1},{1,0},{2,3},{3,2},{4,5},{5,4},{6,7},{7,6},{8,9},{9,8},{10,11... | collective-permute-start | bytes 3538952 | tf_op jit(solution)/shard_map/ppermute | solution.py:1010
  172.7 4.6 %collective-permute-start.6 = (bf16[2,2,4,48,768]{4,3,2,1,0:T(8,128)(2,1)}, bf16[2,2,4,48,768]{4,3,2,1,0:T(8,128)(2,1)}, u32[]{:S(2)}, u32[]{:S(2)}) collective-permute-start(bf16[2,2,4,48,768]{4,3,2,1,0:T(8,128)(2,1)} %get-tuple-element.103), channel_id=1, source_target_pairs={{0,1},{1,0},{2,3},{3,2},{4,5},{5,4},{6,7},{7,6},{8,9},{9,8},{10,11... | collective-permute-start | bytes 3538952 | tf_op jit(solution)/shard_map/ppermute | solution.py:1010
  173.0 35.5 %all-to-all-start.2 = ((bf16[32,32,576]{2,1,0:T(8,128)(2,1)}), bf16[32,32,576]{2,1,0:T(8,128)(2,1)S(1)}, u32[]{:S(2)}, u32[]{:S(2)}) async-start(bf16[32,32,576]{2,1,0:T(8,128)(2,1)} %get-tuple-element.122), calls=%async_computation.2 | async-start | bytes 2621440 | tf_op jit(solution)/shard_map/all_to_all | solution.py:1210
  191.4 3.1 %collective-permute-start.7 = (bf16[2,2,4,48,768]{4,3,2,1,0:T(8,128)(2,1)}, bf16[2,2,4,48,768]{4,3,2,1,0:T(8,128)(2,1)S(1)}, u32[]{:S(2)}, u32[]{:S(2)}) collective-permute-start(bf16[2,2,4,48,768]{4,3,2,1,0:T(8,128)(2,1)} %get-tuple-element.108), channel_id=1, source_target_pairs={{0,1},{1,0},{2,3},{3,2},{4,5},{5,4},{6,7},{7,6},{8,9},{9,8},{10,11... | collective-permute-start | bytes 3538952 | tf_op jit(solution)/shard_map/ppermute | solution.py:1010
  191.8 4.5 %collective-permute-start.8 = (bf16[2,2,4,48,768]{4,3,2,1,0:T(8,128)(2,1)}, bf16[2,2,4,48,768]{4,3,2,1,0:T(8,128)(2,1)S(1)}, u32[]{:S(2)}, u32[]{:S(2)}) collective-permute-start(bf16[2,2,4,48,768]{4,3,2,1,0:T(8,128)(2,1)} %get-tuple-element.110), channel_id=1, source_target_pairs={{0,1},{1,0},{2,3},{3,2},{4,5},{5,4},{6,7},{7,6},{8,9},{9,8},{10,11... | collective-permute-start | bytes 3538952 | tf_op jit(solution)/shard_map/ppermute | solution.py:1010
  192.0 26.9 %collective-permute-start.9 = (bf16[2,4,48,768]{3,2,1,0:T(8,128)(2,1)}, bf16[2,4,48,768]{3,2,1,0:T(8,128)(2,1)}, u32[]{:S(2)}, u32[]{:S(2)}) collective-permute-start(bf16[2,4,48,768]{3,2,1,0:T(8,128)(2,1)} %get-tuple-element.127), channel_id=1, source_target_pairs={{0,16},{1,17},{2,18},{3,19},{4,20},{5,21},{6,22},{7,23},{8,24},{9,... | collective-permute-start | bytes 1769480 | tf_op jit(solution)/shard_map/ppermute | solution.py:1010
  192.8 26.1 %collective-permute-start.10 = (bf16[2,4,48,768]{3,2,1,0:T(8,128)(2,1)}, bf16[2,4,48,768]{3,2,1,0:T(8,128)(2,1)}, u32[]{:S(2)}, u32[]{:S(2)}) collective-permute-start(bf16[2,4,48,768]{3,2,1,0:T(8,128)(2,1)} %get-tuple-element.129), channel_id=1, source_target_pairs={{0,2},{1,3},{2,0},{3,1},{4,6},{5,7},{6,4},{7,5},{8,10},{9,11},{10,... | collective-permute-start | bytes 1769480 | tf_op jit(solution)/shard_map/ppermute | solution.py:1010
  196.2 1.3 copy-start
  197.5 1.3 copy-start.1
  200.4 0.8 copy-start.4
  201.3 23.4 %collective-permute-start.11 = (bf16[2,4,48,768]{3,2,1,0:T(8,128)(2,1)}, bf16[2,4,48,768]{3,2,1,0:T(8,128)(2,1)}, u32[]{:S(2)}, u32[]{:S(2)}) collective-permute-start(bf16[2,4,48,768]{3,2,1,0:T(8,128)(2,1)} %bitcast.21), channel_id=1, source_target_pairs={{0,16},{1,17},{2,18},{3,19},{4,20},{5,21},{6,22},{7,23},{8,24},{9,... | collective-permute-start | bytes 1769480 | tf_op jit(solution)/shard_map/ppermute | solution.py:1010
  202.0 23.0 %collective-permute-start.12 = (bf16[2,4,48,768]{3,2,1,0:T(8,128)(2,1)}, bf16[2,4,48,768]{3,2,1,0:T(8,128)(2,1)}, u32[]{:S(2)}, u32[]{:S(2)}) collective-permute-start(bf16[2,4,48,768]{3,2,1,0:T(8,128)(2,1)} %bitcast.23), channel_id=1, source_target_pairs={{0,2},{1,3},{2,0},{3,1},{4,6},{5,7},{6,4},{7,5},{8,10},{9,11},{10,... | collective-permute-start | bytes 1769480 | tf_op jit(solution)/shard_map/ppermute | solution.py:1010
  209.6 9.3 %copy-start.2 = (bf16[2,4,48,768]{3,2,1,0:T(8,128)(2,1)S(1)}, bf16[2,4,48,768]{3,2,1,0:T(8,128)(2,1)}, u32[]{:S(2)}) copy-start(bf16[2,4,48,768]{3,2,1,0:T(8,128)(2,1)} %get-tuple-element.126.a_own) | copy-start | bytes 1769476
  209.6 9.3 %copy-start.3 = (bf16[2,4,48,768]{3,2,1,0:T(8,128)(2,1)S(1)}, bf16[2,4,48,768]{3,2,1,0:T(8,128)(2,1)}, u32[]{:S(2)}) copy-start(bf16[2,4,48,768]{3,2,1,0:T(8,128)(2,1)} %get-tuple-element.128.b_own) | copy-start | bytes 1769476
  218.9 6.1 %copy-start.5 = (bf16[8,48,768]{2,1,0:T(8,128)(2,1)S(1)}, bf16[8,48,768]{2,1,0:T(8,128)(2,1)}, u32[]{:S(2)}) copy-start(bf16[8,48,768]{2,1,0:T(8,128)(2,1)} %copy-done.4) | copy-start | bytes 1769476
  220.5 10.7 %collective-permute-start.13 = (bf16[4,48,768]{2,1,0:T(8,128)(2,1)S(1)}, bf16[4,48,768]{2,1,0:T(8,128)(2,1)S(1)}, u32[]{:S(2)}, u32[]{:S(2)}) collective-permute-start(bf16[4,48,768]{2,1,0:T(8,128)(2,1)S(1)} %get-tuple-element.131), channel_id=1, source_target_pairs={{0,2},{1,3},{2,0},{3,1},{4,6},{5,7},{6,4},{7,5},{8,10},{9,11},{10,... | collective-permute-start | bytes 884744 | tf_op jit(solution)/shard_map/ppermute | solution.py:1010
  222.1 9.6 %collective-permute-start.14 = (bf16[4,48,768]{2,1,0:T(8,128)(2,1)S(1)}, bf16[4,48,768]{2,1,0:T(8,128)(2,1)S(1)}, u32[]{:S(2)}, u32[]{:S(2)}) collective-permute-start(bf16[4,48,768]{2,1,0:T(8,128)(2,1)S(1)} %get-tuple-element.133), channel_id=1, source_target_pairs={{0,16},{1,17},{2,18},{3,19},{4,20},{5,21},{6,22},{7,23},{8,24},{9,... | collective-permute-start | bytes 884744 | tf_op jit(solution)/shard_map/ppermute | solution.py:1010
  226.6 10.0 %collective-permute-start.15 = (bf16[4,48,768]{2,1,0:T(8,128)(2,1)S(1)}, bf16[4,48,768]{2,1,0:T(8,128)(2,1)S(1)}, u32[]{:S(2)}, u32[]{:S(2)}) collective-permute-start(bf16[4,48,768]{2,1,0:T(8,128)(2,1)S(1)} %get-tuple-element.137), channel_id=1, source_target_pairs={{0,2},{1,3},{2,0},{3,1},{4,6},{5,7},{6,4},{7,5},{8,10},{9,11},{10,... | collective-permute-start | bytes 884744 | tf_op jit(solution)/shard_map/ppermute | solution.py:1010
  227.6 9.0 %collective-permute-start.16 = (bf16[4,48,768]{2,1,0:T(8,128)(2,1)S(1)}, bf16[4,48,768]{2,1,0:T(8,128)(2,1)S(1)}, u32[]{:S(2)}, u32[]{:S(2)}) collective-permute-start(bf16[4,48,768]{2,1,0:T(8,128)(2,1)S(1)} %get-tuple-element.139), channel_id=1, source_target_pairs={{0,16},{1,17},{2,18},{3,19},{4,20},{5,21},{6,22},{7,23},{8,24},{9,... | collective-permute-start | bytes 884744 | tf_op jit(solution)/shard_map/ppermute | solution.py:1010
  231.9 10.4 %collective-permute-start.17 = (bf16[2,48,1536]{2,1,0:T(8,128)(2,1)S(1)}, bf16[2,48,1536]{2,1,0:T(8,128)(2,1)S(1)}, u32[]{:S(2)}, u32[]{:S(2)}) collective-permute-start(bf16[2,48,1536]{2,1,0:T(8,128)(2,1)S(1)} %get-tuple-element.145), channel_id=1, source_target_pairs={{0,4},{1,5},{2,6},{3,7},{4,0},{5,1},{6,2},{7,3},{8,12},{9,13},{10,... | collective-permute-start | bytes 884744 | tf_op jit(solution)/shard_map/ppermute | solution.py:1010
  236.7 9.2 %collective-permute-start.18 = (bf16[2,48,1536]{2,1,0:T(8,128)(2,1)S(1)}, bf16[2,48,1536]{2,1,0:T(8,128)(2,1)S(1)}, u32[]{:S(2)}, u32[]{:S(2)}) collective-permute-start(bf16[2,48,1536]{2,1,0:T(8,128)(2,1)S(1)} %get-tuple-element.149), channel_id=1, source_target_pairs={{0,4},{1,5},{2,6},{3,7},{4,0},{5,1},{6,2},{7,3},{8,12},{9,13},{10,... | collective-permute-start | bytes 884744 | tf_op jit(solution)/shard_map/ppermute | solution.py:1010
  238.7 13.9 %all-to-all-start.3 = ((f32[32,8,128]{2,1,0:T(8,128)}), f32[32,8,128]{2,1,0:T(8,128)S(1)}, u32[]{:S(2)}, u32[]{:S(2)}) async-start(f32[32,8,128]{2,1,0:T(8,128)} %get-tuple-element.140), calls=%async_computation.3 | async-start | bytes 262144 | tf_op jit(solution)/shard_map/all_to_all | solution.py:1238
  242.3 16.5 %collective-permute-start.20 = (bf16[48,1536]{1,0:T(8,128)(2,1)S(1)}, bf16[48,1536]{1,0:T(8,128)(2,1)S(1)}, u32[]{:S(2)}, u32[]{:S(2)}) collective-permute-start(bf16[48,1536]{1,0:T(8,128)(2,1)S(1)} %get-tuple-element.152), channel_id=1, source_target_pairs={{0,8},{1,9},{2,10},{3,11},{4,12},{5,13},{6,14},{7,15},{8,0},{9,1},... | collective-permute-start | bytes 442376 | tf_op jit(solution)/shard_map/ppermute | solution.py:1010
  245.9 15.5 %collective-permute-start.19 = (bf16[48,1536]{1,0:T(8,128)(2,1)S(1)}, bf16[48,1536]{1,0:T(8,128)(2,1)S(1)}, u32[]{:S(2)}, u32[]{:S(2)}) collective-permute-start(bf16[48,1536]{1,0:T(8,128)(2,1)S(1)} %get-tuple-element.155), channel_id=1, source_target_pairs={{0,8},{1,9},{2,10},{3,11},{4,12},{5,13},{6,14},{7,15},{8,0},{9,1},... | collective-permute-start | bytes 442376 | tf_op jit(solution)/shard_map/ppermute | solution.py:1010
  252.7 9.5 %copy-start.9 = (f32[8,128]{1,0:T(8,128)}, f32[8,128]{1,0:T(8,128)S(1)}, u32[]{:S(2)}) copy-start(f32[8,128]{1,0:T(8,128)S(1)} %reduce_sum.28) | copy-start | bytes 12292
Sparse Core Ops, SparseCore 0:
  10.9 108.2 all-gather.2
